TPU v7x, 256 devices: a whole 4x4x8 slice. The times are simulated.
256 devices in a mesh: dir: 8 (over z), row: 32 (over x, y, core).
Axes of the slice: x: 4, y: 4, z: 8, core: 2. Of those that a mesh axis runs over, the one named last changes fastest.
Arguments:
- influence: bfloat16 [3, 128, 192, 144], P(None, 'row'), may hold values from -0.5 to 0.5
- foot_rows: int32 [8, 3, 128], P('dir', None, 'row'), may hold values from 0 to 127, as said below
- foot_columns: int32 [8, 3, 160], P('dir'), may hold values from 0 to 191
- actuator_codes: int32 [3, 48, 48], replicated, may hold values from 0 to 8191, as said below
- poke_rows: int32 [2048], replicated, may hold values from 0 to 8191, as said below
- subaperture_valid: int32 [8, 64, 80], P('dir', 'row'), may hold values 0 or 1
Outputs:
- interaction: bfloat16 [6912, 8, 10240], P(('dir', 'row'))
Inputs may be any that keep to these rules, and one draw needn't show every extreme that they name: `foot_rows`: for every direction, mirror and pupil row y the surface row lies within 2 rows of y, and in every draw some lie exactly 2 rows above and some exactly 2 rows below their pupil row. `actuator_codes`: all entries are distinct. `poke_rows`: all entries are distinct.
All inputs are finite; a program needn't handle non-finite values. No bound on the sum of `subaperture_valid` on one device may be relied on, other than what follows from the above.
Results may differ from a plain program's by a relative error of at most 0.01.
Values may be sent and summed in bfloat16 or wider, within the bound.
A program may use at most 64 MiB of HBM per device.

v0:
```python
import jax
import jax.numpy as jnp
from jax import lax
from jax.sharding import PartitionSpec as P

NAR = 48
NA = 48
BAND = 3


def shifted(block, axis, distance):
    devices = range(lax.axis_size(axis))
    route = [(i - distance, i) for i in devices if i - distance in devices]
    return lax.ppermute(block, axis, route)


def parity_sign(code_values, row_values):
    folded = jnp.bitwise_and(code_values, row_values)
    for stride in (16, 8, 4, 2, 1):
        folded = jnp.bitwise_xor(folded, jnp.right_shift(folded, stride))
    return (1 - 2 * jnp.bitwise_and(folded, 1)).astype(jnp.bfloat16)


def pick_codes(code_table, positions):
    return code_table[positions]


def shards(influence, foot_rows, foot_columns, actuator_codes, poke_rows, subaperture_valid):
    mirrors = influence.shape[0]
    shard_rows = influence.shape[1]
    surface_rows = shard_rows * lax.axis_size("row")
    base_row = lax.axis_index("row") * shard_rows
    received = []
    for offset in (1, -1):
        received.append(shifted(influence, "row", offset))
    window = jnp.concatenate([received[0], influence, received[1]], axis=1)
    window_rows = window.shape[1]
    local_rows = foot_rows[0] - base_row + shard_rows
    pick_rows = (
        local_rows[:, :, None] == jnp.arange(window_rows, dtype=jnp.int32)[None, None, :]
    ).astype(jnp.bfloat16)
    flat_window = window.reshape(mirrors, window_rows, -1)
    row_picked = jnp.einsum(
        "kyw,kwz->kyz", pick_rows, flat_window, preferred_element_type=jnp.float32
    ).astype(jnp.bfloat16)
    row_picked = row_picked.reshape(mirrors, shard_rows, window.shape[2], window.shape[3])
    pick_columns = (
        foot_columns[0][:, :, None] == jnp.arange(window.shape[2], dtype=jnp.int32)[None, None, :]
    ).astype(jnp.bfloat16)
    sampled = jnp.einsum(
        "kxc,kyca->kyxa", pick_columns, row_picked, preferred_element_type=jnp.float32
    ).astype(jnp.bfloat16)
    band_start = jnp.clip(foot_rows[0] * NAR // surface_rows - 1, 0, NAR - BAND)
    slot_index = jnp.arange(BAND * NA, dtype=jnp.int32)
    code_index = band_start[:, :, None] * NA + slot_index[None, None, :]
    flat_codes = actuator_codes.reshape(mirrors, -1)
    column_code = jax.vmap(pick_codes)(flat_codes, code_index)
    commands = parity_sign(column_code[..., None], poke_rows[None, None, None, :])
    surface = jnp.einsum(
        "kyxa,kyap->kyxp", sampled, commands, preferred_element_type=jnp.float32
    ).astype(jnp.bfloat16)
    pupil_phase = jnp.sum(surface.astype(jnp.float32), axis=0)
    subaperture_rows = shard_rows // 2
    blocks = pupil_phase.reshape(
        subaperture_rows, 2, pupil_phase.shape[1] // 2, 2, pupil_phase.shape[2]
    )
    slope_across = 0.5 * (
        blocks[:, 0, :, 1] - blocks[:, 0, :, 0] + (blocks[:, 1, :, 1] - blocks[:, 1, :, 0])
    )
    slope_down = 0.5 * (
        blocks[:, 1, :, 0] - blocks[:, 0, :, 0] + (blocks[:, 1, :, 1] - blocks[:, 0, :, 1])
    )
    valid_mask = subaperture_valid[0].astype(jnp.float32)[:, None, :, None]
    slopes = (jnp.stack([slope_across, slope_down], axis=1) * valid_mask).astype(jnp.bfloat16)
    slope_rows = slopes.reshape(-1, slopes.shape[-1])
    norm_factor = poke_rows.shape[0] ** (-0.5)
    all_codes = actuator_codes.reshape(-1)
    sign_table = parity_sign(all_codes[:, None], poke_rows[None, :])
    decoded = lax.dot_general(
        sign_table, slope_rows, (((1,), (1,)), ((), ())), preferred_element_type=jnp.float32
    )
    decoded = (decoded * norm_factor).astype(jnp.bfloat16)[:, None, :]
    return lax.all_to_all(
        lax.all_to_all(decoded, "dir", split_axis=0, concat_axis=1, tiled=True),
        "row",
        split_axis=0,
        concat_axis=2,
        tiled=True,
    )


def solution(mesh):
    return jax.shard_map(
        shards,
        mesh=mesh,
        in_specs=(
            P(None, "row", None, None),
            P("dir", None, "row"),
            P("dir", None, None),
            P(),
            P(),
            P("dir", "row", None),
        ),
        out_specs=P(("dir", "row"), None, None),
        check_vma=False,
    )
```

profile of v0, /device:TPU:1, one launch (start us, length us, event | category | flops | bytes accessed | tf_op | source)
XLA Modules:
  0.0 348.3 jit_solution(8696664589740996872)
XLA Ops:
  0.0 4.6 %collective-permute-start = (bf16[3,4,192,144]{2,3,1,0:T(8,128)(2,1)}, bf16[3,4,192,144]{2,3,1,0:T(8,128)(2,1)S(1)}, u32[]{:S(2)}, u32[]{:S(2)}) collective-permute-start(bf16[3,4,192,144]{2,3,1,0:T(8,128)(2,1)} %param.6), channel_id=1, source_target_pairs={{0,1},{1,2},{2,3},{3,4},{4,5},{5,6},{6,7},{7,8},{8,9},{9,10},{10,1... | collective-permute-start | bytes 1990664 | tf_op jit(solution)/shard_map/ppermute | solution.py:14
  4.6 1.9 collective-permute-start.1
  12.6 14.4 %gather_fusion = s32[1728]{0:T(1024)S(1)} fusion(s32[3,2304]{1,0:T(4,128)S(1)} %reshape.169, s32[1728]{0:T(1024)S(1)} %reshape.171), kind=kCustom, calls=%fused_computation | custom fusion | bytes 27648 | tf_op jit(solution)/shard_map/vmap()/gather | solution.py:25
  27.2 2.0 pad_maximum_fusion
  29.1 3.4 copy.86
  32.5 6.7 %reshape.167 = bf16[3,12,27648]{2,1,0:T(8,128)(2,1)} reshape(bf16[3,12,192,144]{3,2,1,0:T(8,128)(2,1)S(1)} %copy.86) | data formatting | bytes 3981312 | tf_op jit(solution)/shard_map/reshape | solution.py:42
  39.2 2.4 convolution_convert_fusion
  41.6 2.0 reshape.168
  43.6 11.2 %convert_reduce_fusion = f32[4,160,2048]{2,1,0:T(8,128)} fusion(s32[2048]{0:T(1024)S(1)} %copy-done.3, s32[3,4,144]{2,1,0:T(4,128)S(1)} %reshape.174, bf16[3,4,192,144]{3,2,1,0:T(8,128)(2,1)S(1)} %reshape.168, s32[3,160]{1,0:T(4,128)S(1)} %bitcast.74), kind=kOutput, calls=%fused_computation.17 | convolution fusion | flops 1302568960 | bytes 5923456 | tf_op jit(solution)/shard_map/kyxa,kyap->kyxp/dot_general | solution.py:59
  54.8 7.5 %reshape.170 = f32[2,2,80,2,2048]{4,3,2,1,0:T(2,128)} reshape(f32[4,160,2048]{2,1,0:T(8,128)} %convert_reduce_fusion) | data formatting | bytes 10485760 | tf_op jit(solution)/shard_map/reshape | solution.py:64
  62.3 8.2 %fusion.57 = (f32[2,1,80,1,2048]{4,3,2,1,0:T(1,128)S(1)}, f32[2,1,80,1,2048]{4,3,2,1,0:T(1,128)S(1)}, f32[2,1,80,1,2048]{4,3,2,1,0:T(1,128)S(1)}, f32[2,1,80,1,2048]{4,3,2,1,0:T(1,128)S(1)}) fusion(f32[2,2,80,2,2048]{4,3,2,1,0:T(2,128)} %reshape.170), kind=kLoop, calls=%fused_computation.79 | loop fusion | bytes 10485760 | tf_op jit(solution)/shard_map/slice | solution.py:68
  70.5 2.5 fusion.31
  73.0 2.5 multiply_bitcast_fusion
  76.6 34.6 %fusion.16 = bf16[6912,1,320]{0,2,1:T(8,128)(2,1)} fusion(bf16[320,2048]{1,0:T(8,128)(2,1)S(1)} %fusion.30, s32[2048]{0:T(1024)S(1)} %copy-done.3, s32[6912]{0:T(1024)S(1)} %copy-done.1), kind=kOutput, calls=%fused_computation.24 | convolution fusion | flops 9276456960 | bytes 5770240 | tf_op jit(solution)/shard_map/dot_general | solution.py:79
  111.7 7.0 %reduce = bf16[6912,320]{0,1:T(8,128)(2,1)} reduce(bf16[6912,1,320]{0,2,1:T(8,128)(2,1)} %fusion.16, bf16[]{:T(256)} %broadcast.200), dimensions={1}, to_apply=%copy.97.reduce_sub_computation | reduce | bytes 8847362 | tf_op jit(solution)/shard_map/broadcast_in_dim | solution.py:82
  118.7 7.5 %copy.140 = bf16[6912,320]{1,0:T(8,128)(2,1)} copy(bf16[6912,320]{0,1:T(8,128)(2,1)} %reduce) | data formatting | bytes 8847360
  126.2 9.6 %reshape.179 = bf16[8,2,138240]{2,1,0:T(2,128)(2,1)} reshape(bf16[6912,320]{1,0:T(8,128)(2,1)} %copy.140) | data formatting | bytes 8847360
  135.8 108.4 %all_to_all.36 = bf16[8,2,138240]{2,1,0:T(2,128)(2,1)} all-to-all(bf16[8,2,138240]{2,1,0:T(2,128)(2,1)} %reshape.179), channel_id=1, replica_groups=mesh['dir'=8,'row'=32] {'dir'}, dimensions={0} | all-to-all | bytes 8847360 | tf_op jit(solution)/shard_map/all_to_all | solution.py:84
  244.3 11.9 %reshape.180 = bf16[6912,1,320]{2,1,0:T(2,128)(2,1)} reshape(bf16[8,2,138240]{2,1,0:T(2,128)(2,1)} %all_to_all.36) | data formatting | bytes 8847360
  256.2 4.9 %copy.108 = bf16[6912,1,320]{2,0,1:T(8,128)(2,1)S(1)} copy(bf16[6912,1,320]{2,1,0:T(2,128)(2,1)} %reshape.180) | data formatting | bytes 8847360
  261.1 1.9 copy.99
  263.1 71.8 %all_to_all.37 = bf16[864,8,320]{2,1,0:T(8,128)(2,1)S(1)} all-to-all(bf16[864,8,320]{2,1,0:T(8,128)(2,1)S(1)} %copy.99), channel_id=1, replica_groups=mesh['dir'=8,'row'=32] {'row'}, dimensions={0} | all-to-all | bytes 8847360 | tf_op jit(solution)/shard_map/all_to_all | solution.py:83
  334.8 3.3 copy.100
  338.2 10.1 %all_to_all.33 = bf16[27,8,10240]{2,1,0:T(8,128)(2,1)} reshape(bf16[27,8,32,320]{3,2,1,0:T(8,128)(2,1)} %copy.100) | data formatting | bytes 8847360 | tf_op jit(solution)/shard_map/all_to_all | solution.py:83
  (26 shorter events, 7.8 us)
Async XLA Ops:
  0.0 27.1 %collective-permute-start = (bf16[3,4,192,144]{2,3,1,0:T(8,128)(2,1)}, bf16[3,4,192,144]{2,3,1,0:T(8,128)(2,1)S(1)}, u32[]{:S(2)}, u32[]{:S(2)}) collective-permute-start(bf16[3,4,192,144]{2,3,1,0:T(8,128)(2,1)} %param.6), channel_id=1, source_target_pairs={{0,1},{1,2},{2,3},{3,4},{4,5},{5,6},{6,7},{7,8},{8,9},{9,10},{10,1... | collective-permute-start | bytes 1990664 | tf_op jit(solution)/shard_map/ppermute | solution.py:14
  4.6 22.6 %collective-permute-start.1 = (bf16[3,4,192,144]{2,3,1,0:T(8,128)(2,1)}, bf16[3,4,192,144]{2,3,1,0:T(8,128)(2,1)S(1)}, u32[]{:S(2)}, u32[]{:S(2)}) collective-permute-start(bf16[3,4,192,144]{2,3,1,0:T(8,128)(2,1)} %param.6), channel_id=1, source_target_pairs={{1,0},{2,1},{3,2},{4,3},{5,4},{6,5},{7,6},{8,7},{9,8},{10,9},{11,1... | collective-permute-start | bytes 1990664 | tf_op jit(solution)/shard_map/ppermute | solution.py:14
  12.6 14.5 %copy-start = (bf16[3,4,192,144]{2,3,1,0:T(8,128)(2,1)S(1)}, bf16[3,4,192,144]{2,3,1,0:T(8,128)(2,1)}, u32[]{:S(2)}) copy-start(bf16[3,4,192,144]{2,3,1,0:T(8,128)(2,1)} %param.6) | copy-start | bytes 1990660
  39.2 4.4 %copy-start.2 = (s32[1,3,160]{2,1,0:T(4,128)S(1)}, s32[1,3,160]{2,1,0:T(4,128)}, u32[]{:S(2)}) copy-start(s32[1,3,160]{2,1,0:T(4,128)} %copy.138) | copy-start | bytes 5764
  39.2 4.4 %copy-start.3 = (s32[2048]{0:T(1024)S(1)}, s32[2048]{0:T(1024)}, u32[]{:S(2)}) copy-start(s32[2048]{0:T(1024)} %param.10) | copy-start | bytes 24580
  75.8 0.8 copy-start.1
where the time goes:
time: 350 us; the launch traced here: 348 us
  blocking collectives  180 us (51%)
  local copies, waits for them, and re-layouts  97.3 us (28%)
  matrix products  48.2 us (14%)
  other arithmetic  15.9 us (5%)
  starting transfers between devices  6.5 us (2%)
    all_to_all x1, blocking collectives, shards(): lax.all_to_all(decoded, 'dir', split_axis=0, concat_axis=1, tiled=True)  108 us
    all_to_all x1, blocking collectives, shards(): lax.all_to_all(lax.all_to_all(decoded, 'dir', split_axis=0, concat_axis=1...  71.8 us
    unnamed x14, local copies, waits for them, and re-layouts  36.1 us
    dot_general x1, matrix products, shards(): lax.dot_general(sign_table, slope_rows, (((1,), (1,)), ((), ())), preferr...  34.6 us
    gather x3, local copies, waits for them, and re-layouts, pick_codes(): return code_table[positions]  14.6 us
    all_to_all x2, local copies, waits for them, and re-layouts, shards(): lax.all_to_all(lax.all_to_all(decoded, 'dir', split_axis=0, concat_axis=1...  13.5 us
    dot_general x1, matrix products, shards(): jnp.einsum('kyxa,kyap->kyxp', sampled, commands, preferred_element_type=j...  11.2 us
    slice x1, local copies, waits for them, and re-layouts, shards(): blocks[:, 0, :, 1] - blocks[:, 0, :, 0]  8.15 us
  transfers between devices with their start and end apart: 2, of which 0 were waited for; matrix products, arithmetic and copies ran while one was open for 6% of the time, Pallas kernels for 0%

commit v1 on v0

v1 whole, which is shorter than its diff:
```python
import functools

import jax
import jax.numpy as jnp
from jax import lax
from jax.experimental import pallas as pl
from jax.experimental.pallas import tpu as pltpu
from jax.sharding import PartitionSpec as P

NAR = 48
NA = 48
BAND = 3
REACH = 2
SPAN = 7
MESH = pl.DeviceIdType.MESH
ANY = pl.BlockSpec(memory_space=pl.ANY)
VMEM = pl.BlockSpec(memory_space=pltpu.VMEM)
SMEM = pl.BlockSpec(memory_space=pltpu.SMEM)


def sign_of(code_values, row_values):
    odd = jnp.bitwise_and(lax.population_count(jnp.bitwise_and(code_values, row_values)), 1)
    return jnp.where(odd == 0, 1.0, -1.0).astype(jnp.bfloat16)


def gram_kernel(n_dir, n_row, mine, pokes_lane, pokes_col, local, own, feet, cols,
                gram, partner, above, below, all_feet, all_cols,
                left, right, halo_send, halo_recv, pair_send, pair_recv,
                feet_send, feet_recv, cols_send, cols_recv):
    me_dir, me = lax.axis_index("dir"), lax.axis_index("row")
    core = lax.rem(me, 2)
    chip = me - core

    def row_of(step):
        return lax.rem(me + step + n_row, n_row)

    def other_core():
        return chip + 1 - core

    barrier = pltpu.get_barrier_semaphore()
    up_from = lax.rem(chip - 1 + n_row, n_row)
    down_from = lax.rem(chip + 2, n_row)
    for source in (up_from, down_from):
        pl.semaphore_signal(barrier, inc=1, device_id=(me_dir, source), device_id_type=MESH)
    for hop in range(n_dir):
        there = lax.rem(me_dir + hop, n_dir)
        if hop:
            pl.semaphore_signal(barrier, inc=1, device_id=(there, me), device_id_type=MESH)
        pl.semaphore_signal(barrier, inc=1, device_id=(there, other_core()), device_id_type=MESH)
    pl.semaphore_wait(barrier, 2 * n_dir + 1)

    copies = []

    def send(src, dst, send_sem, recv_sem, target):
        copy = pltpu.make_async_remote_copy(
            src_ref=src, dst_ref=dst, send_sem=send_sem, recv_sem=recv_sem,
            device_id=target, device_id_type=MESH,
        )
        copy.start()
        copies.append(copy)

    rows = own.shape[1]
    next_chip = lax.rem(chip + 2, n_row)
    prev_chip = lax.rem(chip - 2 + n_row, n_row)

    def halo(k, slot, to_core):
        edge = own.at[:, pl.ds(rows - REACH, REACH)] if k == 0 else own.at[:, pl.ds(0, REACH)]
        landing = above if k == 0 else below
        target = (next_chip if k == 0 else prev_chip) + to_core
        return pltpu.make_async_remote_copy(
            src_ref=edge, dst_ref=landing, send_sem=halo_send.at[to_core], recv_sem=halo_recv.at[k],
            device_id=(me_dir, target), device_id_type=MESH,
        )

    @pl.when(core == 1)
    def _():
        for to_core in range(2):
            halo(0, 0, to_core).start()

    @pl.when(core == 0)
    def _():
        for to_core in range(2):
            halo(1, 0, to_core).start()

    send(own, partner, pair_send, pair_recv, (me_dir, other_core()))
    for hop in range(n_dir):
        there = lax.rem(me_dir + hop, n_dir)
        if hop:
            send(feet, all_feet.at[core, me_dir], feet_send.at[hop, 0], feet_recv.at[hop, 0], (there, me))
            send(cols, all_cols.at[me_dir], cols_send.at[hop], cols_recv.at[hop], (there, me))
        send(feet, all_feet.at[core, me_dir], feet_send.at[hop, 1], feet_recv.at[hop, 1],
             (there, other_core()))
    local_feet = pltpu.make_async_copy(feet, all_feet.at[core, me_dir], feet_send.at[0, 0])
    local_feet.start()
    local_cols = pltpu.make_async_copy(cols, all_cols.at[me_dir], cols_send.at[0])
    local_cols.start()

    n_mine, n_poke = left.shape
    tile = 48

    @pl.loop(0, n_mine // tile)
    def _(step):
        at = pl.ds(pl.multiple_of(step * tile, tile), tile)
        left[at, :] = sign_of(mine[at, :], pokes_lane[...])

    high = 128

    @pl.loop(0, n_poke // high)
    def _(step):
        at = pl.ds(pl.multiple_of(step * high, high), high)
        right[at, :] = sign_of(local[...], pokes_col[at, :])

    gram[...] = jnp.dot(left[...], right[...], preferred_element_type=jnp.float32).astype(gram.dtype)

    local_feet.wait()
    local_cols.wait()
    for copy in copies:
        copy.wait()

    @pl.when(core == 1)
    def _():
        for to_core in range(2):
            halo(0, 0, to_core).wait_send()

    @pl.when(core == 0)
    def _():
        for to_core in range(2):
            halo(1, 0, to_core).wait_send()

    halo(0, 0, 0).wait_recv()
    halo(1, 0, 0).wait_recv()


def apply_kernel(feet, place, gram, own, partner, above, below, cols, mask, out,
                 window, sums, weights, staged, sems):
    core = lax.rem(lax.axis_index("row"), 2)
    rows = own.shape[1]
    loads = [
        pltpu.make_async_copy(above, window.at[:, pl.ds(0, REACH)], sems.at[0]),
        pltpu.make_async_copy(own, window.at[:, pl.ds(REACH + rows * core, rows)], sems.at[1]),
        pltpu.make_async_copy(partner, window.at[:, pl.ds(REACH + rows * (1 - core), rows)], sems.at[2]),
        pltpu.make_async_copy(below, window.at[:, pl.ds(REACH + 2 * rows, REACH)], sems.at[3]),
    ]
    for load in loads:
        load.start()
    for load in loads:
        load.wait()
    mirrors, window_rows, slots, columns = window.shape
    n_dir = mask.shape[0]
    wide = cols.shape[-1]
    lane = lax.broadcasted_iota(jnp.int32, (1, wide), 1)
    col_id = lax.broadcasted_iota(jnp.int32, (columns, wide), 0)

    @pl.loop(0, n_dir)
    def _(d):
        sums[...] = jnp.zeros_like(sums)
        for k in range(mirrors):
            for i in range(rows):
                later = cols[d, 8 * k + i, :][None, :]
                first = cols[d, 8 * k + 4 + i, :][None, :]
                turn = jnp.where(lane < 32 * i + 80, -1.0, 1.0)
                odd = jnp.where(col_id == later, 1.0, 0.0) + jnp.where(col_id == first, turn, 0.0)
                even = odd * (-turn)
                for a in range(2):
                    y = 2 * i + a
                    w = feet[y // rows, d, 0, 384 + rows * k + y % rows]
                    part = jnp.dot(
                        window[k, w], (odd if a else even).astype(jnp.bfloat16),
                        preferred_element_type=jnp.float32,
                    )
                    at = pl.ds(pl.multiple_of(place[w] + k * SPAN * NA, NA), slots)
                    sums[at, pl.ds(128 * i, wide)] += part
        weights[...] = sums[...].astype(jnp.bfloat16)
        part = jnp.dot(gram[...], weights[...], preferred_element_type=jnp.float32)
        part = part * mask[d, :][None, :]
        n = staged.shape[1] // n_dir
        for t in range(staged.shape[0]):
            staged[t, pl.ds(d, n, stride=n_dir), :] = part[:, 128 * t : 128 * (t + 1)]

    step = 27

    @pl.loop(0, out.shape[0] // step)
    def _(b):
        for t in range(staged.shape[0]):
            block = staged[t, pl.ds(pl.multiple_of(b * step * n_dir, n_dir), step * n_dir), :]
            block = block.reshape(step, n_dir, 128).astype(out.dtype)
            out[pl.ds(b * step, step), :, 128 * t : 128 * (t + 1)] = block


AROUND = (
    (0, 1), (1, 0), (0, 3), (3, 0), (1, 1), (3, 3), (1, 3), (3, 1),
    (2, 1), (1, 2), (2, 3), (3, 2), (0, 2), (2, 0), (2, 2),
)


def exchange_kernel(pieces, decoded, out, send_sem, recv_sem, keep_sem):
    me_dir, me = lax.axis_index("dir"), lax.axis_index("row")
    core = lax.rem(me, 2)
    chip = me // 2
    x, y = chip // 4, lax.rem(chip, 4)
    each = decoded.shape[0] // 16
    lanes = decoded.shape[2]

    def chip_at(dx, dy):
        return lax.rem(x + dx, 4) * 4 + lax.rem(y + dy, 4)

    barrier = pltpu.get_barrier_semaphore()
    for dx, dy in AROUND:
        pl.semaphore_signal(
            barrier, inc=1, device_id=(me_dir, chip_at(dx, dy) * 2 + core), device_id_type=MESH
        )
    pl.semaphore_wait(barrier, len(AROUND))

    columns = pl.ds(pl.multiple_of(chip * lanes, 128), lanes)
    keep = pltpu.make_async_copy(decoded.at[pl.ds(chip * each, each)], out.at[:, :, columns], keep_sem)
    keep.start()
    size = each // pieces

    def copy(n, piece, order):
        dx, dy = AROUND[n] if order == 0 else AROUND[n][::-1]
        there = chip_at(dx, dy)
        return pltpu.make_async_remote_copy(
            src_ref=decoded.at[pl.ds(there * each + piece * size, size)],
            dst_ref=out.at[pl.ds(piece * size, size), :, columns],
            send_sem=send_sem.at[n, piece], recv_sem=recv_sem.at[n, piece],
            device_id=(me_dir, there * 2 + core), device_id_type=MESH,
        )

    for order in range(2):
        @pl.when(core == order)
        def _(order=order):
            for piece in range(pieces):
                for n in range(len(AROUND)):
                    copy(n, piece, order).start()

    keep.wait()
    for piece in range(pieces):
        for n in range(len(AROUND)):
            copy(n, piece, 0).wait()


def shards(influence, foot_rows, foot_columns, actuator_codes, poke_rows, subaperture_valid):
    mirrors, shard_rows, columns, slots = influence.shape
    n_dir, n_row = lax.axis_size("dir"), lax.axis_size("row")
    surface_rows = shard_rows * n_row
    me_dir, me = lax.axis_index("dir"), lax.axis_index("row")
    core, chip = me % 2, me // 2
    chip_rows = 2 * shard_rows
    first_row = chip * chip_rows - REACH
    subs = subaperture_valid.shape[2]
    acts = actuator_codes.size
    n_poke = poke_rows.shape[0]
    each = acts // (n_dir * n_row)
    mine = 16 * each
    wide = 256

    later, first = foot_columns[0, :, 1::2], foot_columns[0, :, 0::2]

    def windows(index):
        both = jnp.concatenate([index, index], axis=1)
        return jnp.stack(
            [jnp.pad(both, ((0, 0), (32 * i, 96 - 32 * i)), constant_values=-1) for i in range(4)],
            axis=1,
        )

    cols = jnp.concatenate([windows(later), windows(first)], axis=1).reshape(mirrors * 8, wide)
    valid = jnp.broadcast_to(subaperture_valid[0][:, None, :], (shard_rows // 2, 2, subs)).reshape(-1)
    window_rows = chip_rows + 2 * REACH
    local_rows = jnp.clip(foot_rows[0] - first_row, 0, window_rows - 1).reshape(-1)
    feet = jnp.concatenate(
        [valid, jnp.zeros((64,), jnp.int32), local_rows, jnp.zeros((116,), jnp.int32)]
    ).reshape(1, 512)

    def band_of(row):
        return jnp.clip(row * NAR // surface_rows - 1, 0, NAR - BAND)

    band_base = jnp.clip(first_row * NAR // surface_rows - 1, 0, NAR - SPAN)
    place = (band_of(first_row + jnp.arange(window_rows, dtype=jnp.int32)) - band_base) * NA
    place = jnp.clip(place, 0, (SPAN - BAND) * NA)
    mine_codes = lax.dynamic_slice(
        actuator_codes.reshape(n_dir, 16, 2, each), (me_dir, 0, core, 0), (1, 16, 1, each)
    ).reshape(mine, 1)
    local_codes = lax.dynamic_slice_in_dim(actuator_codes, band_base, SPAN, axis=1).reshape(1, -1)
    n_local = mirrors * SPAN * NA
    own = influence.transpose(0, 1, 3, 2)

    bf16, i32, f32 = jnp.bfloat16, jnp.int32, jnp.float32
    dma = pltpu.SemaphoreType.DMA
    gram, partner, above, below, all_feet, all_cols = pl.pallas_call(
        functools.partial(gram_kernel, n_dir, n_row),
        out_shape=(
            jax.ShapeDtypeStruct((mine, n_local), bf16),
            jax.ShapeDtypeStruct(own.shape, bf16),
            jax.ShapeDtypeStruct((mirrors, REACH, slots, columns), bf16),
            jax.ShapeDtypeStruct((mirrors, REACH, slots, columns), bf16),
            jax.ShapeDtypeStruct((2, n_dir, 1, 512), i32),
            jax.ShapeDtypeStruct((n_dir, mirrors * 8, wide), i32),
        ),
        in_specs=[VMEM, VMEM, VMEM, VMEM, ANY, ANY, ANY],
        out_specs=(VMEM, ANY, ANY, ANY, ANY, ANY),
        scratch_shapes=[
            pltpu.VMEM((mine, n_poke), bf16),
            pltpu.VMEM((n_poke, n_local), bf16),
            dma((2,)), dma((2,)), dma, dma,
            dma((n_dir, 2)), dma((n_dir, 2)), dma((n_dir,)), dma((n_dir,)),
        ],
        compiler_params=pltpu.CompilerParams(
            collective_id=0, has_side_effects=True, vmem_limit_bytes=48 << 20
        ),
        name="gram",
    )(mine_codes, poke_rows.reshape(1, -1), poke_rows.reshape(-1, 1), local_codes, own, feet, cols)

    lanes = 2 * (shard_rows // 2) * 2 * subs
    scale = 0.5 * n_poke ** (-0.5)
    mask = all_feet[:, :, 0, : lanes // 2].transpose(1, 0, 2).reshape(n_dir, lanes)
    mask = mask.astype(f32) * scale
    decoded = pl.pallas_call(
        apply_kernel,
        out_shape=jax.ShapeDtypeStruct((mine, n_dir, lanes), bf16),
        in_specs=[SMEM, SMEM, VMEM, ANY, ANY, ANY, ANY, VMEM, VMEM],
        out_specs=VMEM,
        scratch_shapes=[
            pltpu.VMEM((mirrors, window_rows, slots, columns), bf16),
            pltpu.VMEM((n_local, lanes), f32),
            pltpu.VMEM((n_local, lanes), bf16),
            pltpu.VMEM((lanes // 128, mine * n_dir, 128), f32),
            dma((4,)),
        ],
        compiler_params=pltpu.CompilerParams(vmem_limit_bytes=56 << 20),
        name="apply",
    )(all_feet, place, gram, own, partner, above, below, all_cols, mask)

    pieces = 3
    return pl.pallas_call(
        functools.partial(exchange_kernel, pieces),
        out_shape=jax.ShapeDtypeStruct((each, n_dir, lanes * 16), bf16),
        in_specs=[ANY],
        out_specs=ANY,
        scratch_shapes=[dma((15, pieces)), dma((15, pieces)), dma],
        compiler_params=pltpu.CompilerParams(collective_id=1, has_side_effects=True),
        name="exchange",
    )(decoded)


def solution(mesh):
    return jax.shard_map(
        shards,
        mesh=mesh,
        in_specs=(
            P(None, "row", None, None),
            P("dir", None, "row"),
            P("dir", None, None),
            P(),
            P(),
            P("dir", "row", None),
        ),
        out_specs=P(("dir", "row"), None, None),
        check_vma=False,
    )
```

time: 350 us -> 123 us (0.35)
  blocking collectives: 180 us -> 0 us
  Pallas kernels: 0 us -> 103 us
  local copies, waits for them, and re-layouts: 97.3 us -> 17.7 us
  matrix products: 48.2 us -> 0 us
  other arithmetic: 15.9 us -> 1.49 us
  starting transfers between devices: 6.5 us -> 0 us
    all_to_all x2 -> x0, blocking collectives: 180 us -> none  [the longest x1 108 us: shards(): lax.all_to_all(decoded, 'dir', split_axis=0, concat_axis=1, tiled=True)]
    pallas_call x0 -> x3, Pallas kernels: none -> 103 us  [the longest x1 55.4 us: shards(): pl.pallas_call(functools.partial(exchange_kernel, pieces), out_shape=jax....]
    dot_general x3 -> x0, matrix products: 48.2 us -> none  [the longest x1 34.6 us: shards(): lax.dot_general(sign_table, slope_rows, (((1,), (1,)), ((), ())), preferr...]
    unnamed x14 -> x27, local copies, waits for them, and re-layouts: 36.1 us -> 11.2 us
    all_to_all x3 -> x0, local copies, waits for them, and re-layouts: 15.4 us -> none  [the longest x2 13.5 us: shards(): lax.all_to_all(lax.all_to_all(decoded, 'dir', split_axis=0, concat_axis=1...]
    reshape x4 -> x5, local copies, waits for them, and re-layouts: 17.2 us -> 2.47 us  [the longest x1 1.13 us: shards(): actuator_codes.reshape(n_dir, 16, 2, each)]
    gather x3 -> x0, local copies, waits for them, and re-layouts: 14.6 us -> none  [pick_codes(): return code_table[positions]]
    broadcast_in_dim x1 -> x0, other arithmetic: 6.97 us -> none  [shards(): decoded = (decoded * norm_factor).astype(jnp.bfloat16)[:, None, :]]
  transfers between devices with their start and end apart: 2 -> 0, of which waited for: 0 -> 0; matrix products, arithmetic and copies ran while one was open for 6% -> 0% of each run, Pallas kernels for 0% -> 0%
where the time goes in v1:
time: 123 us; the launch traced here: 122 us
  Pallas kernels  103 us (84%)
  local copies, waits for them, and re-layouts  17.7 us (14%)
  other arithmetic  1.49 us (1%)
    pallas_call x1, Pallas kernels, shards(): pl.pallas_call(functools.partial(exchange_kernel, pieces), out_shape=jax....  55.4 us
    pallas_call x1, Pallas kernels, shards(): pl.pallas_call(functools.partial(gram_kernel, n_dir, n_row), out_shape=(j...  24.1 us
    pallas_call x1, Pallas kernels, shards(): pl.pallas_call(apply_kernel, out_shape=jax.ShapeDtypeStruct((mine, n_dir,...  23.3 us
    unnamed x27, local copies, waits for them, and re-layouts  11.2 us

profile of v1, /device:TPU:1, one launch (start us, length us, event | category | flops | bytes accessed | tf_op | source)
XLA Modules:
  0.0 122.1 jit_solution(9558909555246524448)
XLA Ops:
  0.0 0.5 multiply_clamp_fusion.place
  0.5 0.7 clamp_reduce_fusion
  1.2 0.1 min.31
  1.3 0.8 slice.10
  2.2 0.9 slice.9
  3.2 0.7 broadcast_in_dim.14
  3.9 0.1 reshape.44
  4.0 0.7 constant_dynamic-slice_fusion
  4.8 0.1 reshape.43.local
  5.4 1.1 reshape.39
  6.6 0.1 reshape.47.mine
  6.7 1.1 copy.15.pokes_col
  7.8 1.2 copy-done
  8.9 0.7 copy-done.7
  9.6 24.1 %gram.1 = (bf16[432,1008]{1,0:T(8,128)(2,1)S(1)}, bf16[3,4,144,192]{3,2,1,0:T(8,128)(2,1)S(1)}, bf16[3,2,144,192]{3,2,1,0:T(8,128)(2,1)S(1)}, bf16[3,2,144,192]{...) custom-call(s32[432,1]{1,0:T(8,128)S(1)} %reshape.47.mine, s32[1,2048]{1,0:T(1,128)S(1)} %bitcast.44, ...), custom_call_target="tpu_custom_call" | custom-call | tf_op jit(solution)/shard_map/gram/pallas_call | solution.py:289
  33.7 0.9 copy-done.1
  34.6 0.9 copy-done.2
  35.6 0.8 copy-done.3
  36.4 0.8 copy-done.4
  37.1 0.7 copy-done.5
  37.9 0.7 mul.32.mask
  38.6 23.3 %apply.1.decoded = bf16[432,8,640]{2,1,0:T(8,128)(2,1)} custom-call(s32[2,8,1,512]{3,2,1,0:T(1,128)} %copy-done.6, s32[12]{0:T(128)} %multiply_clamp_fusion.place, bf16[432,1008]{1,0:T(8,128)(2,1)} %copy-done.1, bf16[3,4,144,192]{3,2,1,0:T(8,128)(2,1)} %bitcast.40, bf16[3,4,144,192]{3,2,1,0:T(8,128)(2,1)} %copy-done.2, bf16[3,2,144,192]{3,2,1,0:T(8,128)(2,1)} %copy-done.3, ...), custom_call_target="tpu_custom_call" | custom-call | tf_op jit(solution)/shard_map/apply/pallas_call | solution.py:317
  61.9 55.4 %exchange.1 = bf16[27,8,10240]{2,1,0:T(8,128)(2,1)} custom-call(bf16[432,8,640]{2,1,0:T(8,128)(2,1)} %apply.1.decoded), custom_call_target="tpu_custom_call" | custom-call | tf_op jit(solution)/shard_map/exchange/pallas_call | solution.py:334
  117.3 4.8 %copy.37 = bf16[27,8,10240]{2,1,0:T(8,128)(2,1)} copy(bf16[27,8,10240]{2,1,0:T(8,128)(2,1)} %exchange.1) | data formatting | bytes 8847360
  (29 shorter events, 0.8 us)
Async XLA Ops:
  7.7 1.2 copy-start
  8.9 0.7 copy-start.7
  33.7 0.9 copy-start.1
  34.6 0.9 copy-start.2
  35.6 0.8 copy-start.3
  36.4 0.8 copy-start.4
  37.1 0.7 copy-start.5
  37.8 0.8 copy-start.6

commit v2 on v1

--- a/solution.py
+++ b/solution.py
@@ -131,75 +131,30 @@
     halo(1, 0, 0).wait_recv()
 
 
-def apply_kernel(feet, place, gram, own, partner, above, below, cols, mask, out,
-                 window, sums, weights, staged, sems):
-    core = lax.rem(lax.axis_index("row"), 2)
-    rows = own.shape[1]
-    loads = [
-        pltpu.make_async_copy(above, window.at[:, pl.ds(0, REACH)], sems.at[0]),
-        pltpu.make_async_copy(own, window.at[:, pl.ds(REACH + rows * core, rows)], sems.at[1]),
-        pltpu.make_async_copy(partner, window.at[:, pl.ds(REACH + rows * (1 - core), rows)], sems.at[2]),
-        pltpu.make_async_copy(below, window.at[:, pl.ds(REACH + 2 * rows, REACH)], sems.at[3]),
-    ]
-    for load in loads:
-        load.start()
-    for load in loads:
-        load.wait()
-    mirrors, window_rows, slots, columns = window.shape
-    n_dir = mask.shape[0]
-    wide = cols.shape[-1]
-    lane = lax.broadcasted_iota(jnp.int32, (1, wide), 1)
-    col_id = lax.broadcasted_iota(jnp.int32, (columns, wide), 0)
-
-    @pl.loop(0, n_dir)
-    def _(d):
-        sums[...] = jnp.zeros_like(sums)
-        for k in range(mirrors):
-            for i in range(rows):
-                later = cols[d, 8 * k + i, :][None, :]
-                first = cols[d, 8 * k + 4 + i, :][None, :]
-                turn = jnp.where(lane < 32 * i + 80, -1.0, 1.0)
-                odd = jnp.where(col_id == later, 1.0, 0.0) + jnp.where(col_id == first, turn, 0.0)
-                even = odd * (-turn)
-                for a in range(2):
-                    y = 2 * i + a
-                    w = feet[y // rows, d, 0, 384 + rows * k + y % rows]
-                    part = jnp.dot(
-                        window[k, w], (odd if a else even).astype(jnp.bfloat16),
-                        preferred_element_type=jnp.float32,
-                    )
-                    at = pl.ds(pl.multiple_of(place[w] + k * SPAN * NA, NA), slots)
-                    sums[at, pl.ds(128 * i, wide)] += part
-        weights[...] = sums[...].astype(jnp.bfloat16)
-        part = jnp.dot(gram[...], weights[...], preferred_element_type=jnp.float32)
-        part = part * mask[d, :][None, :]
-        n = staged.shape[1] // n_dir
-        for t in range(staged.shape[0]):
-            staged[t, pl.ds(d, n, stride=n_dir), :] = part[:, 128 * t : 128 * (t + 1)]
-
-    step = 27
-
-    @pl.loop(0, out.shape[0] // step)
-    def _(b):
-        for t in range(staged.shape[0]):
-            block = staged[t, pl.ds(pl.multiple_of(b * step * n_dir, n_dir), step * n_dir), :]
-            block = block.reshape(step, n_dir, 128).astype(out.dtype)
-            out[pl.ds(b * step, step), :, 128 * t : 128 * (t + 1)] = block
-
-
 AROUND = (
     (0, 1), (1, 0), (0, 3), (3, 0), (1, 1), (3, 3), (1, 3), (3, 1),
     (2, 1), (1, 2), (2, 3), (3, 2), (0, 2), (2, 0), (2, 2),
 )
-
-
-def exchange_kernel(pieces, decoded, out, send_sem, recv_sem, keep_sem):
+PLACE = tuple((3 * w - 6) // 8 + 1 for w in range(12))
+REACHED = ((0, 5), (1, 4), (1, 5), (2, 5))
+
+
+def deliver_kernel(chips, feet, gram, own, partner, above, below, cols, mask, out,
+                   window, frames, sums, weights, staged, ready,
+                   load_sem, send_sem, recv_sem, keep_sem):
     me_dir, me = lax.axis_index("dir"), lax.axis_index("row")
     core = lax.rem(me, 2)
-    chip = me // 2
-    x, y = chip // 4, lax.rem(chip, 4)
-    each = decoded.shape[0] // 16
-    lanes = decoded.shape[2]
+    chip = lax.div(me, 2)
+    x, y = lax.div(chip, 4), lax.rem(chip, 4)
+    rows = own.shape[1]
+    loads = [
+        pltpu.make_async_copy(above, window.at[:, pl.ds(0, REACH)], load_sem.at[0]),
+        pltpu.make_async_copy(own, window.at[:, pl.ds(REACH + rows * core, rows)], load_sem.at[1]),
+        pltpu.make_async_copy(partner, window.at[:, pl.ds(REACH + rows * (1 - core), rows)], load_sem.at[2]),
+        pltpu.make_async_copy(below, window.at[:, pl.ds(REACH + 2 * rows, REACH)], load_sem.at[3]),
+    ]
+    for load in loads:
+        load.start()
 
     def chip_at(dx, dy):
         return lax.rem(x + dx, 4) * 4 + lax.rem(y + dy, 4)
@@ -209,40 +164,114 @@
         pl.semaphore_signal(
             barrier, inc=1, device_id=(me_dir, chip_at(dx, dy) * 2 + core), device_id_type=MESH
         )
-    pl.semaphore_wait(barrier, len(AROUND))
-
-    columns = pl.ds(pl.multiple_of(chip * lanes, 128), lanes)
-    keep = pltpu.make_async_copy(decoded.at[pl.ds(chip * each, each)], out.at[:, :, columns], keep_sem)
-    keep.start()
-    size = each // pieces
-
-    def copy(n, piece, order):
+
+    n_dir = mask.shape[0]
+    mirrors, window_rows, slots, columns = window.shape
+    frame = frames.shape[2]
+    wide = cols.shape[-1]
+    lanes = out.shape[2] // chips
+    each = out.shape[0]
+    lane = lax.broadcasted_iota(jnp.int32, (1, wide), 1)
+    col_id = lax.broadcasted_iota(jnp.int32, (columns, wide), 0)
+
+    frames[...] = jnp.zeros_like(frames)
+    sums[...] = jnp.zeros_like(sums)
+    for load in loads:
+        load.wait()
+    for w in range(window_rows):
+        start = PLACE[w]
+        if 2 <= w <= 4:
+            start = start + 1 - lax.div(chip + chips - 1, chips)
+        if 8 <= w <= 9:
+            start = start - lax.div(chip + 1, chips)
+        at = pl.ds(start * NA if isinstance(start, int) else pl.multiple_of(start * NA, NA), slots)
+        for k in range(mirrors):
+            frames[k, w, at, :] = window[k, w]
+
+    def copy(n, t, order):
         dx, dy = AROUND[n] if order == 0 else AROUND[n][::-1]
         there = chip_at(dx, dy)
         return pltpu.make_async_remote_copy(
-            src_ref=decoded.at[pl.ds(there * each + piece * size, size)],
-            dst_ref=out.at[pl.ds(piece * size, size), :, columns],
-            send_sem=send_sem.at[n, piece], recv_sem=recv_sem.at[n, piece],
+            src_ref=ready.at[t, pl.ds(there * each, each)],
+            dst_ref=out.at[:, :, pl.ds(pl.multiple_of(chip * lanes + 128 * t, 128), 128)],
+            send_sem=send_sem.at[n, t], recv_sem=recv_sem.at[n, t],
             device_id=(me_dir, there * 2 + core), device_id_type=MESH,
         )
 
-    for order in range(2):
-        @pl.when(core == order)
-        def _(order=order):
-            for piece in range(pieces):
+    def keep(t):
+        return pltpu.make_async_copy(
+            ready.at[t, pl.ds(chip * each, each)],
+            out.at[:, :, pl.ds(pl.multiple_of(chip * lanes + 128 * t, 128), 128)],
+            keep_sem.at[t],
+        )
+
+    tiles = lanes // 128
+    for t in range(tiles):
+        if t < tiles - 1:
+            low, many = REACHED[t]
+
+            @pl.loop(0, n_dir)
+            def _(d, t=t, low=low, many=many):
+                block = pl.ds(pl.multiple_of(d * 128, 128), 128)
+                for k in range(mirrors):
+                    later = cols[d, 8 * k + t, :][None, :]
+                    first = cols[d, 8 * k + 4 + t, :][None, :]
+                    turn = jnp.where(lane < 32 * t + 80, -1.0, 1.0)
+                    odd = jnp.where(col_id == later, 1.0, 0.0) + jnp.where(col_id == first, turn, 0.0)
+                    even = odd * (-turn)
+                    part = None
+                    for a in range(2):
+                        y = 2 * t + a
+                        w = feet[y // rows, d, 0, 384 + rows * k + y % rows]
+                        term = jnp.dot(
+                            frames[k, w, pl.ds(low * NA, many * NA), :],
+                            (odd if a else even).astype(jnp.bfloat16),
+                            preferred_element_type=jnp.float32,
+                        )
+                        part = term if part is None else part + term
+                    mine = pl.ds(k * frame + low * NA, many * NA)
+                    whole = pl.ds(k * frame, frame)
+                    sums[mine, block] += part[:, :128]
+                    weights[whole, block] = sums[whole, block].astype(jnp.bfloat16)
+                    sums[whole, block] = jnp.zeros((frame, 128), jnp.float32)
+                    sums[mine, block] = part[:, 128:]
+        else:
+            weights[...] = sums[...].astype(jnp.bfloat16)
+
+        @pl.loop(0, n_dir // 2)
+        def _(c, t=t):
+            part = jnp.dot(
+                gram[...], weights[:, pl.ds(pl.multiple_of(c * 256, 256), 256)],
+                preferred_element_type=jnp.float32,
+            )
+            for e in range(2):
+                d = 2 * c + e
+                scale = mask[d, t, :][None, :]
+                staged[pl.ds(d, gram.shape[0], stride=n_dir), :] = part[:, 128 * e : 128 * (e + 1)] * scale
+
+        @pl.loop(0, chips)
+        def _(b, t=t):
+            block = staged[pl.ds(pl.multiple_of(b * each * n_dir, n_dir), each * n_dir), :]
+            ready[t, pl.ds(b * each, each)] = block.reshape(each, n_dir, 128).astype(ready.dtype)
+
+        if t == 0:
+            pl.semaphore_wait(barrier, len(AROUND))
+        for order in range(2):
+            @pl.when(core == order)
+            def _(order=order, t=t):
                 for n in range(len(AROUND)):
-                    copy(n, piece, order).start()
-
-    keep.wait()
-    for piece in range(pieces):
+                    copy(n, t, order).start()
+        keep(t).start()
+
+    for t in range(tiles):
+        keep(t).wait()
         for n in range(len(AROUND)):
-            copy(n, piece, 0).wait()
+            copy(n, t, 0).wait()
 
 
 def shards(influence, foot_rows, foot_columns, actuator_codes, poke_rows, subaperture_valid):
     mirrors, shard_rows, columns, slots = influence.shape
     n_dir, n_row = lax.axis_size("dir"), lax.axis_size("row")
-    surface_rows = shard_rows * n_row
     me_dir, me = lax.axis_index("dir"), lax.axis_index("row")
     core, chip = me % 2, me // 2
     chip_rows = 2 * shard_rows
@@ -271,16 +300,12 @@
         [valid, jnp.zeros((64,), jnp.int32), local_rows, jnp.zeros((116,), jnp.int32)]
     ).reshape(1, 512)
 
-    def band_of(row):
-        return jnp.clip(row * NAR // surface_rows - 1, 0, NAR - BAND)
-
-    band_base = jnp.clip(first_row * NAR // surface_rows - 1, 0, NAR - SPAN)
-    place = (band_of(first_row + jnp.arange(window_rows, dtype=jnp.int32)) - band_base) * NA
-    place = jnp.clip(place, 0, (SPAN - BAND) * NA)
+    chips = n_row // 2
+    padded = jnp.pad(actuator_codes, ((0, 0), (2, 2), (0, 0)))
     mine_codes = lax.dynamic_slice(
         actuator_codes.reshape(n_dir, 16, 2, each), (me_dir, 0, core, 0), (1, 16, 1, each)
     ).reshape(mine, 1)
-    local_codes = lax.dynamic_slice_in_dim(actuator_codes, band_base, SPAN, axis=1).reshape(1, -1)
+    local_codes = lax.dynamic_slice_in_dim(padded, 3 * chip, SPAN, axis=1).reshape(1, -1)
     n_local = mirrors * SPAN * NA
     own = influence.transpose(0, 1, 3, 2)
 
@@ -305,7 +330,7 @@
             dma((n_dir, 2)), dma((n_dir, 2)), dma((n_dir,)), dma((n_dir,)),
         ],
         compiler_params=pltpu.CompilerParams(
-            collective_id=0, has_side_effects=True, vmem_limit_bytes=48 << 20
+            collective_id=0, has_side_effects=True
         ),
         name="gram",
     )(mine_codes, poke_rows.reshape(1, -1), poke_rows.reshape(-1, 1), local_codes, own, feet, cols)
@@ -313,33 +338,25 @@
     lanes = 2 * (shard_rows // 2) * 2 * subs
     scale = 0.5 * n_poke ** (-0.5)
     mask = all_feet[:, :, 0, : lanes // 2].transpose(1, 0, 2).reshape(n_dir, lanes)
-    mask = mask.astype(f32) * scale
-    decoded = pl.pallas_call(
-        apply_kernel,
-        out_shape=jax.ShapeDtypeStruct((mine, n_dir, lanes), bf16),
-        in_specs=[SMEM, SMEM, VMEM, ANY, ANY, ANY, ANY, VMEM, VMEM],
-        out_specs=VMEM,
+    mask = (mask.astype(f32) * scale).reshape(n_dir, lanes // 128, 128)
+    tiles = lanes // 128
+    return pl.pallas_call(
+        functools.partial(deliver_kernel, chips),
+        out_shape=jax.ShapeDtypeStruct((each, n_dir, lanes * chips), bf16),
+        in_specs=[SMEM, VMEM, ANY, ANY, ANY, ANY, VMEM, VMEM],
+        out_specs=ANY,
         scratch_shapes=[
             pltpu.VMEM((mirrors, window_rows, slots, columns), bf16),
-            pltpu.VMEM((n_local, lanes), f32),
-            pltpu.VMEM((n_local, lanes), bf16),
-            pltpu.VMEM((lanes // 128, mine * n_dir, 128), f32),
-            dma((4,)),
+            pltpu.VMEM((mirrors, window_rows, SPAN * NA, columns), bf16),
+            pltpu.VMEM((n_local, n_dir * 128), f32),
+            pltpu.VMEM((n_local, n_dir * 128), bf16),
+            pltpu.VMEM((mine * n_dir, 128), f32),
+            pltpu.VMEM((tiles, mine, n_dir, 128), bf16),
+            dma((4,)), dma((15, tiles)), dma((15, tiles)), dma((tiles,)),
         ],
-        compiler_params=pltpu.CompilerParams(vmem_limit_bytes=56 << 20),
-        name="apply",
-    )(all_feet, place, gram, own, partner, above, below, all_cols, mask)
-
-    pieces = 3
-    return pl.pallas_call(
-        functools.partial(exchange_kernel, pieces),
-        out_shape=jax.ShapeDtypeStruct((each, n_dir, lanes * 16), bf16),
-        in_specs=[ANY],
-        out_specs=ANY,
-        scratch_shapes=[dma((15, pieces)), dma((15, pieces)), dma],
         compiler_params=pltpu.CompilerParams(collective_id=1, has_side_effects=True),
-        name="exchange",
-    )(decoded)
+        name="deliver",
+    )(all_feet, gram, own, partner, above, below, all_cols, mask)
 
 
 def solution(mesh):

time: 123 us -> 105 us (0.85)
  Pallas kernels: 103 us -> 87.6 us
  local copies, waits for them, and re-layouts: 17.7 us -> 14.6 us
    pallas_call x2 -> x1, Pallas kernels: 78.7 us -> 60.9 us  [shards(): pl.pallas_call(functools.partial(deliver_kernel, chips), out_shape=jax.Sh...]
    unnamed x27 -> x11, local copies, waits for them, and re-layouts: 11.2 us -> 5.24 us
    pallas_call x1, Pallas kernels: 24.1 us -> 26.7 us  [shards(): pl.pallas_call(functools.partial(gram_kernel, n_dir, n_row), out_shape=(j...]
where the time goes in v2:
time: 105 us
  Pallas kernels  87.6 us (83%)
  local copies, waits for them, and re-layouts  14.6 us (14%)
  other arithmetic  2.27 us (2%)
    pallas_call x1, Pallas kernels, shards(): pl.pallas_call(functools.partial(deliver_kernel, chips), out_shape=jax.Sh...  60.9 us
    pallas_call x1, Pallas kernels, shards(): pl.pallas_call(functools.partial(gram_kernel, n_dir, n_row), out_shape=(j...  26.7 us
    unnamed x11, local copies, waits for them, and re-layouts  5.24 us

profile of v2, /device:TPU:1, one launch (start us, length us, event | category | flops | bytes accessed | tf_op | source)
XLA Modules:
  0.0 104.6 jit_solution(10651181190121751194)
XLA Ops:
  0.0 0.7 clamp_reduce_fusion
  0.7 0.1 min.12
  0.8 0.8 slice.10
  1.6 0.9 slice.9
  2.7 0.7 broadcast_in_dim.14
  3.3 0.1 reshape.46
  3.4 0.7 pad_add_fusion.2
  4.1 0.7 pad_dynamic-slice_fusion
  4.8 0.7 reshape.45.local
  5.5 0.1 constant_dynamic-update-slice_fusion.6
  5.6 0.1 constant_dynamic-update-slice_fusion.5
  5.7 0.1 constant_dynamic-update-slice_fusion.4
  5.8 0.1 constant_dynamic-update-slice_fusion.2
  5.8 0.1 constant_dynamic-update-slice_fusion.1
  5.9 0.1 constant_dynamic-update-slice_fusion
  6.0 0.6 copy.26
  6.6 1.1 %reshape.41 = s32[8,16,2,27]{3,2,1,0:T(2,128)S(1)} reshape(s32[3,48,48]{2,1,0:T(8,128)} %param.9) | data formatting | bytes 55296 | tf_op jit(solution)/shard_map/reshape | solution.py:306
  7.8 0.8 reshape.49.mine
  8.6 2.0 %copy.15.pokes_col = s32[2048,1]{1,0:T(8,128)} copy(s32[2048,1]{0,1:T(1,128)} %bitcast.44) | data formatting | bytes 16384 | tf_op jit(solution)/shard_map/reshape | solution.py:336
  10.6 26.7 %gram.1 = (bf16[432,1008]{1,0:T(8,128)(2,1)}, bf16[3,4,144,192]{3,2,1,0:T(8,128)(2,1)}, bf16[3,2,144,192]{3,2,1,0:T(8,128)(2,1)}, bf16[3,2,144,192]{3,2,1,0:T(8,...) custom-call(s32[432,1]{1,0:T(8,128)} %reshape.49.mine, s32[1,2048]{1,0:T(1,128)} %bitcast.45, ...), custom_call_target="tpu_custom_call" | custom-call | tf_op jit(solution)/shard_map/gram/pallas_call | solution.py:314
  37.3 0.8 convert_multiply_fusion
  38.1 0.7 mul.24.mask
  38.8 60.9 %deliver.1 = bf16[27,8,10240]{2,1,0:T(8,128)(2,1)} custom-call(s32[2,8,1,512]{3,2,1,0:T(1,128)} %get-tuple-element.11.feet, bf16[432,1008]{1,0:T(8,128)(2,1)} %get-tuple-element.12.gram, bf16[3,4,144,192]{3,2,1,0:T(8,128)(2,1)} %bitcast.41, bf16[3,4,144,192]{3,2,1,0:T(8,128)(2,1)} %get-tuple-element.13.partner, ...), custom_call_target="tpu_custom_call" | custom-call | tf_op jit(solution)/shard_map/deliver/pallas_call | solution.py:343
  99.8 4.8 %copy.37 = bf16[27,8,10240]{2,1,0:T(8,128)(2,1)} copy(bf16[27,8,10240]{2,1,0:T(8,128)(2,1)} %deliver.1) | data formatting | bytes 8847360
  (11 shorter events, 0.2 us)

commit v3 on v0

v3 whole, which is shorter than its diff:
```python
import functools

import jax
import jax.numpy as jnp
from jax import lax
from jax.experimental import pallas as pl
from jax.experimental.pallas import tpu as pltpu
from jax.sharding import PartitionSpec as P

NAR = 48
NA = 48
REACH = 2
SPAN = 7
MESH = pl.DeviceIdType.MESH
ANY = pl.BlockSpec(memory_space=pl.ANY)
VMEM = pl.BlockSpec(memory_space=pltpu.VMEM)

AROUND = (
    (0, 1), (1, 0), (0, 3), (3, 0), (1, 1), (3, 3), (1, 3), (3, 1),
    (2, 1), (1, 2), (2, 3), (3, 2), (0, 2), (2, 0), (2, 2),
)
PLACE = tuple((3 * w - 6) // 8 + 1 for w in range(12))
REACHED = ((0, 5), (1, 4), (1, 5), (2, 5))
BF16, F32, I32 = jnp.bfloat16, jnp.float32, jnp.int32


def iota(shape, axis):
    return lax.broadcasted_iota(I32, shape, axis)


def over(value, divisor):
    return jnp.right_shift(value * (65536 // divisor + 1), 16)


def sign_of(code_values, row_values):
    odd = jnp.bitwise_and(lax.population_count(jnp.bitwise_and(code_values, row_values)), 1)
    return jnp.where(odd == 0, 1.0, -1.0).astype(BF16)


def dot(a, b):
    return jnp.dot(a, b, preferred_element_type=F32)


def halves(codes):
    return jnp.right_shift(codes, 7).astype(F32).astype(BF16), jnp.bitwise_and(codes, 127).astype(F32).astype(BF16)


def window_kernel(n_dir, n_row, own, foot_rows, foot_cols, valid, codes, pokes_lane, pokes_tile, out,
                  window, frames, sums, weights, staged, ready, left, right, gram, mine, local,
                  feet_land, cols_land, valid_land, feet, cols_mat, valid_mat, picks, mask,
                  far_send, far_recv, halo_send, halo_recv, pair_send, pair_recv,
                  feet_send, feet_recv, cols_send, cols_recv, valid_send, valid_recv, keep_sem, own_sem):
    me_dir, me = lax.axis_index("dir"), lax.axis_index("row")
    core = lax.rem(me, 2)
    chip = lax.div(me, 2)
    chips = n_row // 2
    x, y = lax.div(chip, 4), lax.rem(chip, 4)
    rows = own.shape[1]
    mirrors, window_rows, slots, columns = window.shape
    frame = frames.shape[2]
    lanes = out.shape[2] // chips
    each = out.shape[0]
    tiles = lanes // 128

    def chip_at(dx, dy):
        return lax.rem(x + dx, 4) * 4 + lax.rem(y + dy, 4)

    barrier = pltpu.get_barrier_semaphore()

    def greet(there_dir, there):
        pl.semaphore_signal(barrier, inc=1, device_id=(there_dir, there), device_id_type=MESH)

    greet(me_dir, lax.rem(2 * chip - 1 + n_row, n_row))
    greet(me_dir, lax.rem(2 * chip + 2, n_row))
    for hop in range(n_dir):
        there = lax.rem(me_dir + hop, n_dir)
        if hop:
            greet(there, me)
        greet(there, 2 * chip + 1 - core)
    for dx, dy in AROUND:
        greet(me_dir, chip_at(dx, dy) * 2 + core)

    keeps = [
        pltpu.make_async_copy(own, window.at[:, pl.ds(REACH + rows * core, rows)], own_sem.at[0]),
        pltpu.make_async_copy(foot_rows, feet_land.at[core * n_dir + me_dir], own_sem.at[1]),
        pltpu.make_async_copy(foot_cols, cols_land.at[me_dir], own_sem.at[2]),
        pltpu.make_async_copy(valid, valid_land.at[core * n_dir + me_dir], own_sem.at[3]),
    ]
    for copy in keeps:
        copy.start()

    pl.semaphore_wait(barrier, 2 * n_dir - 1 + 2 + len(AROUND))

    def remote(src, dst, send_sem, recv_sem, target):
        return pltpu.make_async_remote_copy(
            src_ref=src, dst_ref=dst, send_sem=send_sem, recv_sem=recv_sem,
            device_id=target, device_id_type=MESH,
        )

    def halo(k, to_core):
        edge = own.at[:, pl.ds(rows - REACH, REACH)] if k == 0 else own.at[:, pl.ds(0, REACH)]
        landing = window.at[:, pl.ds(0 if k == 0 else REACH + 2 * rows, REACH)]
        target = lax.rem(2 * chip + (2 if k == 0 else n_row - 2), n_row)
        return remote(edge, landing, halo_send.at[to_core], halo_recv.at[k], (me_dir, target + to_core))

    @pl.when(core == 1)
    def _():
        for to_core in range(2):
            halo(0, to_core).start()

    @pl.when(core == 0)
    def _():
        for to_core in range(2):
            halo(1, to_core).start()

    pair = remote(own, window.at[:, pl.ds(REACH + rows * core, rows)], pair_send, pair_recv,
                  (me_dir, 2 * chip + 1 - core))
    pair.start()
    small = []
    for hop in range(n_dir):
        there = lax.rem(me_dir + hop, n_dir)
        for side in range(2):
            if hop == 0 and side == 0:
                continue
            target = (there, me if side == 0 else 2 * chip + 1 - core)
            small.append(remote(foot_rows, feet_land.at[core * n_dir + me_dir],
                                feet_send.at[hop, side], feet_recv.at[hop, side], target))
            small.append(remote(valid, valid_land.at[core * n_dir + me_dir],
                                valid_send.at[hop, side], valid_recv.at[hop, side], target))
        if hop:
            small.append(remote(foot_cols, cols_land.at[me_dir], cols_send.at[hop], cols_recv.at[hop],
                                (there, me)))
    for copy in small:
        copy.start()

    n_mine, n_poke = left.shape
    n_local = right.shape[1]
    table = [halves(codes[k]) for k in range(mirrors)]
    at = iota((n_mine, 1), 0)
    at = at + each * (over(at, each) + core)
    at_row = over(at, NA)
    at_col = at - NA * at_row
    per_dir = mirrors * NAR // n_dir
    upper = jnp.zeros((n_mine, NA), F32)
    lower = jnp.zeros((n_mine, NA), F32)
    for k in range(mirrors):
        hot = (iota((n_mine, NAR), 1) == at_row + (per_dir * me_dir - NAR * k)).astype(F32).astype(BF16)
        upper += dot(hot, table[k][0])
        lower += dot(hot, table[k][1])
    picked = jnp.where(iota((n_mine, NA), 1) == at_col, upper * 128.0 + lower, 0.0)
    mine[...] = jnp.sum(picked, axis=1, keepdims=True).astype(I32)

    lane = iota((1, n_local), 1)
    block = over(lane, NA)
    tile_of = (iota((NA, n_local), 0) == lane - NA * block).astype(F32).astype(BF16)
    row_id = iota((NAR, n_local), 0)
    found = jnp.zeros((1, n_local), F32)
    for k in range(mirrors):
        spread = dot(table[k][0], tile_of) * 128.0 + dot(table[k][1], tile_of)
        wanted = jnp.where((block >= SPAN * k) & (block < SPAN * (k + 1)), block - SPAN * k + 3 * chip - 2, -1)
        found += jnp.sum(jnp.where(row_id == wanted, spread, 0.0), axis=0, keepdims=True)
    local[...] = found.astype(I32)

    turned = jnp.transpose(pokes_tile[...])
    for j in range(n_poke // 128):
        right[128 * j : 128 * (j + 1), :] = sign_of(turned[:, j : j + 1], local[...])

    @pl.loop(0, n_mine // 48)
    def _(step):
        part = pl.ds(pl.multiple_of(step * 48, 48), 48)
        left[part, :] = sign_of(mine[part, :], pokes_lane[...])

    gram[...] = dot(left[...], right[...]).astype(BF16)

    for copy in keeps:
        copy.wait()
    for copy in small:
        copy.wait()
    to_scalar = pltpu.make_async_copy(feet_land, feet, own_sem.at[4])
    to_scalar.start()
    for d in range(n_dir):
        for k in range(mirrors):
            cols_mat[d * mirrors + k : d * mirrors + k + 1, :] = cols_land[d, k]
        for i in range(rows):
            valid_mat[i, d : d + 1, :] = valid_land[i // 2 * n_dir + d, 0, i % 2 : i % 2 + 1, :]
    n_cols = cols_mat.shape[1]
    subs = n_cols // 2
    wide = picks.shape[2]
    cols_value = cols_mat[...].astype(F32).astype(BF16)
    for t in range(4):
        lane = iota((1, wide), 1) - 32 * t
        inside = (lane >= 0) & (lane < n_cols)
        column = 2 * jnp.where(lane >= subs, lane - subs, lane)
        for first in range(2):
            wanted = jnp.where(inside, column + 1 - first, -1)
            hot = (iota((n_cols, wide), 0) == wanted).astype(F32).astype(BF16)
            value = jnp.where(inside, dot(cols_value, hot), -1.0)
            for r in range(n_dir * mirrors):
                picks[(4 * first + t) * n_dir * mirrors + r] = value[r : r + 1, :]
    lane = iota((1, lanes), 1)
    hot = (iota((subs, lanes), 0) == lane - subs * over(lane, subs)).astype(F32).astype(BF16)
    total = jnp.zeros((n_dir, lanes), F32)
    for i in range(rows):
        value = dot(valid_mat[i].astype(F32).astype(BF16), hot)
        total += jnp.where((lane >= n_cols * i) & (lane < n_cols * (i + 1)), value, 0.0)
    total = total * (0.5 * n_poke ** (-0.5))
    for t in range(tiles):
        for d in range(n_dir):
            mask[t * n_dir + d] = total[d : d + 1, 128 * t : 128 * (t + 1)]

    frames[...] = jnp.zeros_like(frames)
    sums[...] = jnp.zeros_like(sums)
    to_scalar.wait()
    pair.wait()

    @pl.when(core == 1)
    def _():
        for to_core in range(2):
            halo(0, to_core).wait_send()

    @pl.when(core == 0)
    def _():
        for to_core in range(2):
            halo(1, to_core).wait_send()

    halo(0, 0).wait_recv()
    halo(1, 0).wait_recv()
    for w in range(window_rows):
        start = PLACE[w]
        if 2 <= w <= 4:
            start = start + 1 - lax.div(chip + chips - 1, chips)
        if 8 <= w <= 9:
            start = start - lax.div(chip + 1, chips)
        part = pl.ds(start * NA if isinstance(start, int) else pl.multiple_of(start * NA, NA), slots)
        for k in range(mirrors):
            frames[k, w, part, :] = window[k, w]

    def far(n, t, order):
        dx, dy = AROUND[n] if order == 0 else AROUND[n][::-1]
        there = chip_at(dx, dy)
        return remote(
            ready.at[t, pl.ds(there * each, each)],
            out.at[:, :, pl.ds(pl.multiple_of(chip * lanes + 128 * t, 128), 128)],
            far_send.at[n, t], far_recv.at[n, t], (me_dir, there * 2 + core),
        )

    def keep(t):
        return pltpu.make_async_copy(
            ready.at[t, pl.ds(chip * each, each)],
            out.at[:, :, pl.ds(pl.multiple_of(chip * lanes + 128 * t, 128), 128)],
            keep_sem.at[t],
        )

    col_id = iota((columns, wide), 0).astype(F32)
    lane = iota((1, wide), 1)
    for t in range(tiles):
        if t < tiles - 1:
            low, many = REACHED[t]
            turn = jnp.where(lane < 32 * t + subs, -1.0, 1.0)

            @pl.loop(0, n_dir)
            def _(d, t=t, low=low, many=many, turn=turn):
                block = pl.ds(pl.multiple_of(d * 128, 128), 128)
                for k in range(mirrors):
                    later = picks[t * n_dir * mirrors + d * mirrors + k]
                    first = picks[(4 + t) * n_dir * mirrors + d * mirrors + k]
                    odd = jnp.where(col_id == later, 1.0, 0.0) + jnp.where(col_id == first, turn, 0.0)
                    even = odd * (-turn)
                    part = None
                    for a in range(2):
                        row = 2 * t + a
                        at = feet[row // rows * n_dir + d, k, 0, row % rows]
                        w = jnp.clip(at - 2 * rows * chip + REACH, 0, window_rows - 1)
                        term = dot(frames[k, w, pl.ds(low * NA, many * NA), :],
                                   (odd if a else even).astype(BF16))
                        part = term if part is None else part + term
                    some = pl.ds(k * frame + low * NA, many * NA)
                    whole = pl.ds(k * frame, frame)
                    sums[some, block] += part[:, :128]
                    weights[whole, block] = sums[whole, block].astype(BF16)
                    sums[whole, block] = jnp.zeros((frame, 128), F32)
                    sums[some, block] = part[:, 128:]
        else:
            weights[...] = sums[...].astype(BF16)

        @pl.loop(0, n_dir // 2)
        def _(c, t=t):
            part = dot(gram[...], weights[:, pl.ds(pl.multiple_of(c * 256, 256), 256)])
            for e in range(2):
                d = 2 * c + e
                staged[pl.ds(d, n_mine, stride=n_dir), :] = part[:, 128 * e : 128 * (e + 1)] * mask[t * n_dir + d]

        @pl.loop(0, chips)
        def _(b, t=t):
            block = staged[pl.ds(pl.multiple_of(b * each * n_dir, n_dir), each * n_dir), :]
            ready[t, pl.ds(b * each, each)] = block.reshape(each, n_dir, 128).astype(BF16)

        for order in range(2):
            @pl.when(core == order)
            def _(order=order, t=t):
                for n in range(len(AROUND)):
                    far(n, t, order).start()
        keep(t).start()

    for t in range(tiles):
        keep(t).wait()
        for n in range(len(AROUND)):
            far(n, t, 0).wait()


def shards(influence, foot_rows, foot_columns, actuator_codes, poke_rows, subaperture_valid):
    mirrors, shard_rows, columns, slots = influence.shape
    n_dir, n_row = lax.axis_size("dir"), lax.axis_size("row")
    chips = n_row // 2
    window_rows = 2 * shard_rows + 2 * REACH
    subs = subaperture_valid.shape[2]
    n_poke = poke_rows.shape[0]
    each = actuator_codes.size // (n_dir * n_row)
    n_mine = chips * each
    n_local = mirrors * SPAN * NA
    lanes = 2 * shard_rows * subs
    tiles = lanes // 128
    dma = pltpu.SemaphoreType.DMA
    return pl.pallas_call(
        functools.partial(window_kernel, n_dir, n_row),
        out_shape=jax.ShapeDtypeStruct((each, n_dir, lanes * chips), BF16),
        in_specs=[ANY, ANY, ANY, ANY, VMEM, VMEM, VMEM],
        out_specs=ANY,
        scratch_shapes=[
            pltpu.VMEM((mirrors, window_rows, slots, columns), BF16),
            pltpu.VMEM((mirrors, window_rows, SPAN * NA, columns), BF16),
            pltpu.VMEM((n_local, n_dir * 128), F32),
            pltpu.VMEM((n_local, n_dir * 128), BF16),
            pltpu.VMEM((n_mine * n_dir, 128), F32),
            pltpu.VMEM((tiles, n_mine, n_dir, 128), BF16),
            pltpu.VMEM((n_mine, n_poke), BF16),
            pltpu.VMEM((n_poke, n_local), BF16),
            pltpu.VMEM((n_mine, n_local), BF16),
            pltpu.VMEM((n_mine, 1), I32),
            pltpu.VMEM((1, n_local), I32),
            pltpu.VMEM((2 * n_dir, mirrors, 1, shard_rows), I32),
            pltpu.VMEM((n_dir, mirrors, 1, 2 * subs), I32),
            pltpu.VMEM((2 * n_dir, 1, shard_rows // 2, subs), I32),
            pltpu.SMEM((2 * n_dir, mirrors, 1, shard_rows), I32),
            pltpu.VMEM((n_dir * mirrors, 2 * subs), I32),
            pltpu.VMEM((shard_rows, n_dir, subs), I32),
            pltpu.VMEM((8 * n_dir * mirrors, 1, 256), F32),
            pltpu.VMEM((tiles * n_dir, 1, 128), F32),
            dma((15, tiles)), dma((15, tiles)), dma((2,)), dma((2,)), dma, dma,
            dma((n_dir, 2)), dma((n_dir, 2)), dma((n_dir,)), dma((n_dir,)),
            dma((n_dir, 2)), dma((n_dir, 2)), dma((tiles,)), dma((5,)),
        ],
        compiler_params=pltpu.CompilerParams(collective_id=0, has_side_effects=True),
        name="window",
    )(
        influence.transpose(0, 1, 3, 2),
        foot_rows.reshape(mirrors, 1, shard_rows),
        foot_columns.reshape(mirrors, 1, 2 * subs),
        subaperture_valid,
        actuator_codes,
        poke_rows.reshape(1, -1),
        poke_rows.reshape(-1, 128),
    )


def solution(mesh):
    return jax.shard_map(
        shards,
        mesh=mesh,
        in_specs=(
            P(None, "row", None, None),
            P("dir", None, "row"),
            P("dir", None, None),
            P(),
            P(),
            P("dir", "row", None),
        ),
        out_specs=P(("dir", "row"), None, None),
        check_vma=False,
    )
```

time: 350 us -> 89.3 us (0.26)
  blocking collectives: 180 us -> 0 us
  local copies, waits for them, and re-layouts: 97.3 us -> 4.82 us
  Pallas kernels: 0 us -> 84.3 us
  matrix products: 48.2 us -> 0 us
  other arithmetic: 15.9 us -> 0 us
  starting transfers between devices: 6.5 us -> 0 us
    all_to_all x2 -> x0, blocking collectives: 180 us -> none  [the longest x1 108 us: shards(): lax.all_to_all(decoded, 'dir', split_axis=0, concat_axis=1, tiled=True)]
    pallas_call x0 -> x1, Pallas kernels: none -> 84.3 us  [shards(): pl.pallas_call(functools.partial(window_kernel, n_dir, n_row), out_shape=...]
    dot_general x3 -> x0, matrix products: 48.2 us -> none  [the longest x1 34.6 us: shards(): lax.dot_general(sign_table, slope_rows, (((1,), (1,)), ((), ())), preferr...]
    unnamed x14 -> x1, local copies, waits for them, and re-layouts: 36.1 us -> 4.82 us
    reshape x4 -> x0, local copies, waits for them, and re-layouts: 17.2 us -> none  [the longest x1 7.54 us: shards(): pupil_phase.reshape(subaperture_rows, 2, pupil_phase.shape[1] // 2, 2, pu...]
    all_to_all x3 -> x0, local copies, waits for them, and re-layouts: 15.4 us -> none  [the longest x2 13.5 us: shards(): lax.all_to_all(lax.all_to_all(decoded, 'dir', split_axis=0, concat_axis=1...]
    gather x3 -> x0, local copies, waits for them, and re-layouts: 14.6 us -> none  [pick_codes(): return code_table[positions]]
    slice x1 -> x0, local copies, waits for them, and re-layouts: 8.15 us -> none  [shards(): blocks[:, 0, :, 1] - blocks[:, 0, :, 0]]
  transfers between devices with their start and end apart: 2 -> 0, of which waited for: 0 -> 0; matrix products, arithmetic and copies ran while one was open for 6% -> 0% of each run, Pallas kernels for 0% -> 0%
where the time goes in v3:
time: 89.3 us; the launch traced here: 89.1 us
  Pallas kernels  84.3 us (94%)
  local copies, waits for them, and re-layouts  4.82 us (5%)
    pallas_call x1, Pallas kernels, shards(): pl.pallas_call(functools.partial(window_kernel, n_dir, n_row), out_shape=...  84.3 us
    unnamed x1, local copies, waits for them, and re-layouts  4.82 us

profile of v3, /device:TPU:1, one launch (start us, length us, event | category | flops | bytes accessed | tf_op | source)
XLA Modules:
  0.0 89.1 jit_solution(5775286738769223788)
XLA Ops:
  0.0 84.3 %window.1 = bf16[27,8,10240]{2,1,0:T(8,128)(2,1)} custom-call(bf16[3,4,144,192]{3,2,1,0:T(8,128)(2,1)} %bitcast.5, s32[3,1,4]{2,1,0:T(1,128)} %bitcast.9, s32[3,1,160]{2,1,0:T(1,128)} %bitcast.8, s32[1,2,80]{2,1,0:T(2,128)} %valid.1, s32[3,48,48]{2,1,0:T(8,128)} %codes.1, s32[1,2048]{1,0:T(1,128)} %bitcast.6, s32[16,128]{1,0:T(8,128)} %bitcast.7), custom_call_target="tpu_custom_call" | custom-call | tf_op jit(solution)/shard_map/window/pallas_call | solution.py:324
  84.3 4.8 %copy.8 = bf16[27,8,10240]{2,1,0:T(8,128)(2,1)} copy(bf16[27,8,10240]{2,1,0:T(8,128)(2,1)} %window.1) | data formatting | bytes 8847360

commit v4 on v3

--- a/solution.py
+++ b/solution.py
@@ -48,7 +48,7 @@
 def window_kernel(n_dir, n_row, own, foot_rows, foot_cols, valid, codes, pokes_lane, pokes_tile, out,
                   window, frames, sums, weights, staged, ready, left, right, gram, mine, local,
                   feet_land, cols_land, valid_land, feet, cols_mat, valid_mat, picks, mask,
-                  far_send, far_recv, halo_send, halo_recv, pair_send, pair_recv,
+                  poke_cols, far_send, far_recv, halo_send, halo_recv, pair_send, pair_recv, relay_send, relay_recv,
                   feet_send, feet_recv, cols_send, cols_recv, valid_send, valid_recv, keep_sem, own_sem):
     me_dir, me = lax.axis_index("dir"), lax.axis_index("row")
     core = lax.rem(me, 2)
@@ -70,13 +70,14 @@
     def greet(there_dir, there):
         pl.semaphore_signal(barrier, inc=1, device_id=(there_dir, there), device_id_type=MESH)
 
-    greet(me_dir, lax.rem(2 * chip - 1 + n_row, n_row))
-    greet(me_dir, lax.rem(2 * chip + 2, n_row))
+    beside = lax.rem(2 * chip + 3 * core - 1 + n_row, n_row)
+    twin = 2 * chip + 1 - core
+    greet(me_dir, beside)
     for hop in range(n_dir):
         there = lax.rem(me_dir + hop, n_dir)
         if hop:
             greet(there, me)
-        greet(there, 2 * chip + 1 - core)
+        greet(there, twin)
     for dx, dy in AROUND:
         greet(me_dir, chip_at(dx, dy) * 2 + core)
 
@@ -87,50 +88,6 @@
         pltpu.make_async_copy(valid, valid_land.at[core * n_dir + me_dir], own_sem.at[3]),
     ]
     for copy in keeps:
-        copy.start()
-
-    pl.semaphore_wait(barrier, 2 * n_dir - 1 + 2 + len(AROUND))
-
-    def remote(src, dst, send_sem, recv_sem, target):
-        return pltpu.make_async_remote_copy(
-            src_ref=src, dst_ref=dst, send_sem=send_sem, recv_sem=recv_sem,
-            device_id=target, device_id_type=MESH,
-        )
-
-    def halo(k, to_core):
-        edge = own.at[:, pl.ds(rows - REACH, REACH)] if k == 0 else own.at[:, pl.ds(0, REACH)]
-        landing = window.at[:, pl.ds(0 if k == 0 else REACH + 2 * rows, REACH)]
-        target = lax.rem(2 * chip + (2 if k == 0 else n_row - 2), n_row)
-        return remote(edge, landing, halo_send.at[to_core], halo_recv.at[k], (me_dir, target + to_core))
-
-    @pl.when(core == 1)
-    def _():
-        for to_core in range(2):
-            halo(0, to_core).start()
-
-    @pl.when(core == 0)
-    def _():
-        for to_core in range(2):
-            halo(1, to_core).start()
-
-    pair = remote(own, window.at[:, pl.ds(REACH + rows * core, rows)], pair_send, pair_recv,
-                  (me_dir, 2 * chip + 1 - core))
-    pair.start()
-    small = []
-    for hop in range(n_dir):
-        there = lax.rem(me_dir + hop, n_dir)
-        for side in range(2):
-            if hop == 0 and side == 0:
-                continue
-            target = (there, me if side == 0 else 2 * chip + 1 - core)
-            small.append(remote(foot_rows, feet_land.at[core * n_dir + me_dir],
-                                feet_send.at[hop, side], feet_recv.at[hop, side], target))
-            small.append(remote(valid, valid_land.at[core * n_dir + me_dir],
-                                valid_send.at[hop, side], valid_recv.at[hop, side], target))
-        if hop:
-            small.append(remote(foot_cols, cols_land.at[me_dir], cols_send.at[hop], cols_recv.at[hop],
-                                (there, me)))
-    for copy in small:
         copy.start()
 
     n_mine, n_poke = left.shape
@@ -163,7 +120,52 @@
 
     turned = jnp.transpose(pokes_tile[...])
     for j in range(n_poke // 128):
-        right[128 * j : 128 * (j + 1), :] = sign_of(turned[:, j : j + 1], local[...])
+        poke_cols[j] = turned[:, j : j + 1]
+    frames[...] = jnp.zeros_like(frames)
+
+    pl.semaphore_wait(barrier, 2 * n_dir + len(AROUND))
+
+    def remote(src, dst, send_sem, recv_sem, target):
+        return pltpu.make_async_remote_copy(
+            src_ref=src, dst_ref=dst, send_sem=send_sem, recv_sem=recv_sem,
+            device_id=target, device_id_type=MESH,
+        )
+
+    far_edge = REACH + 2 * rows
+    halo = remote(own.at[:, pl.ds((rows - REACH) * core, REACH)],
+                  window.at[:, pl.ds(far_edge * (1 - core), REACH)], halo_send, halo_recv, (me_dir, beside))
+    halo.start()
+    pair = [
+        remote(own.at[k], window.at[k, pl.ds(REACH + rows * core, rows)], pair_send.at[k], pair_recv.at[k],
+               (me_dir, twin))
+        for k in range(mirrors)
+    ]
+    for copy in pair:
+        copy.start()
+    small = []
+    for hop in range(n_dir):
+        there = lax.rem(me_dir + hop, n_dir)
+        for side in range(2):
+            if hop == 0 and side == 0:
+                continue
+            target = (there, me if side == 0 else twin)
+            small.append(remote(foot_rows, feet_land.at[core * n_dir + me_dir],
+                                feet_send.at[hop, side], feet_recv.at[hop, side], target))
+            small.append(remote(valid, valid_land.at[core * n_dir + me_dir],
+                                valid_send.at[hop, side], valid_recv.at[hop, side], target))
+        if hop:
+            small.append(remote(foot_cols, cols_land.at[me_dir], cols_send.at[hop], cols_recv.at[hop],
+                                (there, me)))
+    for copy in small:
+        copy.start()
+
+    @pl.loop(0, n_poke // 128)
+    def _(j):
+        part = pl.ds(pl.multiple_of(j * 128, 128), 128)
+        right[part, :] = sign_of(poke_cols[j], local[...])
+
+    relay = remote(window.at[:, pl.ds(far_edge * core, REACH)], window.at[:, pl.ds(far_edge * core, REACH)],
+                   relay_send, relay_recv, (me_dir, twin))
 
     @pl.loop(0, n_mine // 48)
     def _(step):
@@ -186,17 +188,17 @@
     n_cols = cols_mat.shape[1]
     subs = n_cols // 2
     wide = picks.shape[2]
-    cols_value = cols_mat[...].astype(F32).astype(BF16)
-    for t in range(4):
+    def pick(t):
         lane = iota((1, wide), 1) - 32 * t
         inside = (lane >= 0) & (lane < n_cols)
         column = 2 * jnp.where(lane >= subs, lane - subs, lane)
         for first in range(2):
             wanted = jnp.where(inside, column + 1 - first, -1)
             hot = (iota((n_cols, wide), 0) == wanted).astype(F32).astype(BF16)
-            value = jnp.where(inside, dot(cols_value, hot), -1.0)
+            value = jnp.where(inside, dot(cols_mat[...].astype(F32).astype(BF16), hot), -1.0)
             for r in range(n_dir * mirrors):
-                picks[(4 * first + t) * n_dir * mirrors + r] = value[r : r + 1, :]
+                picks[first * n_dir * mirrors + r] = value[r : r + 1, :]
+
     lane = iota((1, lanes), 1)
     hot = (iota((subs, lanes), 0) == lane - subs * over(lane, subs)).astype(F32).astype(BF16)
     total = jnp.zeros((n_dir, lanes), F32)
@@ -208,32 +210,22 @@
         for d in range(n_dir):
             mask[t * n_dir + d] = total[d : d + 1, 128 * t : 128 * (t + 1)]
 
-    frames[...] = jnp.zeros_like(frames)
-    sums[...] = jnp.zeros_like(sums)
     to_scalar.wait()
-    pair.wait()
-
-    @pl.when(core == 1)
-    def _():
-        for to_core in range(2):
-            halo(0, to_core).wait_send()
-
-    @pl.when(core == 0)
-    def _():
-        for to_core in range(2):
-            halo(1, to_core).wait_send()
-
-    halo(0, 0).wait_recv()
-    halo(1, 0).wait_recv()
-    for w in range(window_rows):
-        start = PLACE[w]
-        if 2 <= w <= 4:
-            start = start + 1 - lax.div(chip + chips - 1, chips)
-        if 8 <= w <= 9:
-            start = start - lax.div(chip + 1, chips)
-        part = pl.ds(start * NA if isinstance(start, int) else pl.multiple_of(start * NA, NA), slots)
-        for k in range(mirrors):
-            frames[k, w, part, :] = window[k, w]
+    for copy in pair:
+        copy.wait()
+
+    def fill(some):
+        for w in some:
+            start = PLACE[w]
+            if 2 <= w <= 4:
+                start = start + 1 - lax.div(chip + chips - 1, chips)
+            if 8 <= w <= 9:
+                start = start - lax.div(chip + 1, chips)
+            part = pl.ds(start * NA if isinstance(start, int) else pl.multiple_of(start * NA, NA), slots)
+            for k in range(mirrors):
+                frames[k, w, part, :] = window[k, w]
+
+    fill(range(REACH, far_edge))
 
     def far(n, t, order):
         dx, dy = AROUND[n] if order == 0 else AROUND[n][::-1]
@@ -253,54 +245,78 @@
 
     col_id = iota((columns, wide), 0).astype(F32)
     lane = iota((1, wide), 1)
-    for t in range(tiles):
-        if t < tiles - 1:
-            low, many = REACHED[t]
-            turn = jnp.where(lane < 32 * t + subs, -1.0, 1.0)
-
-            @pl.loop(0, n_dir)
-            def _(d, t=t, low=low, many=many, turn=turn):
-                block = pl.ds(pl.multiple_of(d * 128, 128), 128)
-                for k in range(mirrors):
-                    later = picks[t * n_dir * mirrors + d * mirrors + k]
-                    first = picks[(4 + t) * n_dir * mirrors + d * mirrors + k]
-                    odd = jnp.where(col_id == later, 1.0, 0.0) + jnp.where(col_id == first, turn, 0.0)
-                    even = odd * (-turn)
-                    part = None
-                    for a in range(2):
-                        row = 2 * t + a
-                        at = feet[row // rows * n_dir + d, k, 0, row % rows]
-                        w = jnp.clip(at - 2 * rows * chip + REACH, 0, window_rows - 1)
-                        term = dot(frames[k, w, pl.ds(low * NA, many * NA), :],
-                                   (odd if a else even).astype(BF16))
-                        part = term if part is None else part + term
-                    some = pl.ds(k * frame + low * NA, many * NA)
-                    whole = pl.ds(k * frame, frame)
-                    sums[some, block] += part[:, :128]
-                    weights[whole, block] = sums[whole, block].astype(BF16)
-                    sums[whole, block] = jnp.zeros((frame, 128), F32)
-                    sums[some, block] = part[:, 128:]
-        else:
-            weights[...] = sums[...].astype(BF16)
-
+    def sample(i):
+        low, many = REACHED[i]
+        turn = jnp.where(lane < 32 * i + subs, -1.0, 1.0)
+        pick(i)
+
+        def framed(value):
+            blank = [jnp.zeros((n * NA, 128), F32) for n in (low, SPAN - low - many)]
+            pieces = [blank[0], value, blank[1]]
+            return jnp.concatenate([p for p in pieces if p.shape[0]], axis=0)
+
+        @pl.loop(0, n_dir)
+        def _(d):
+            block = pl.ds(pl.multiple_of(d * 128, 128), 128)
+            for k in range(mirrors):
+                later = picks[d * mirrors + k]
+                first = picks[(n_dir + d) * mirrors + k]
+                hot = jnp.where(col_id == later, 1.0, 0.0) + jnp.where(col_id == first, turn, 0.0)
+                hot = hot.astype(BF16)
+                terms = []
+                for a in range(2):
+                    row = 2 * i + a
+                    at = feet[row // rows * n_dir + d, k, 0, row % rows]
+                    w = jnp.clip(at - 2 * rows * chip + REACH, 0, window_rows - 1)
+                    terms.append(dot(frames[k, w, pl.ds(low * NA, many * NA), :], hot))
+                part = terms[1] - terms[0] * turn
+                whole = pl.ds(k * frame, frame)
+                here, after = framed(part[:, :128]), framed(part[:, 128:])
+                if i == 1:
+                    sums[0, whole, block] = here
+                    sums[1, whole, block] = after
+                elif i == 0:
+                    weights[whole, block] = here.astype(BF16)
+                    sums[0, whole, block] += after
+                else:
+                    weights[whole, block] = (here + sums[1, whole, block]).astype(BF16)
+                    sums[1, whole, block] = after
+
+    def deliver(t):
         @pl.loop(0, n_dir // 2)
-        def _(c, t=t):
+        def _(c):
             part = dot(gram[...], weights[:, pl.ds(pl.multiple_of(c * 256, 256), 256)])
             for e in range(2):
                 d = 2 * c + e
                 staged[pl.ds(d, n_mine, stride=n_dir), :] = part[:, 128 * e : 128 * (e + 1)] * mask[t * n_dir + d]
 
         @pl.loop(0, chips)
-        def _(b, t=t):
+        def _(b):
             block = staged[pl.ds(pl.multiple_of(b * each * n_dir, n_dir), each * n_dir), :]
             ready[t, pl.ds(b * each, each)] = block.reshape(each, n_dir, 128).astype(BF16)
 
         for order in range(2):
             @pl.when(core == order)
-            def _(order=order, t=t):
+            def _(order=order):
                 for n in range(len(AROUND)):
                     far(n, t, order).start()
         keep(t).start()
+
+    sample(1)
+    halo.wait()
+    relay.start()
+    sample(2)
+    deliver(2)
+    relay.wait()
+    fill((0, 1, far_edge, far_edge + 1))
+    sample(0)
+    deliver(0)
+    weights[...] = sums[0].astype(BF16)
+    deliver(1)
+    sample(3)
+    deliver(3)
+    weights[...] = sums[1].astype(BF16)
+    deliver(4)
 
     for t in range(tiles):
         keep(t).wait()
@@ -323,13 +339,13 @@
     dma = pltpu.SemaphoreType.DMA
     return pl.pallas_call(
         functools.partial(window_kernel, n_dir, n_row),
-        out_shape=jax.ShapeDtypeStruct((each, n_dir, lanes * chips), BF16),
+        out_shape=pltpu.VMEM((each, n_dir, lanes * chips), BF16),
         in_specs=[ANY, ANY, ANY, ANY, VMEM, VMEM, VMEM],
-        out_specs=ANY,
+        out_specs=VMEM,
         scratch_shapes=[
             pltpu.VMEM((mirrors, window_rows, slots, columns), BF16),
             pltpu.VMEM((mirrors, window_rows, SPAN * NA, columns), BF16),
-            pltpu.VMEM((n_local, n_dir * 128), F32),
+            pltpu.VMEM((2, n_local, n_dir * 128), F32),
             pltpu.VMEM((n_local, n_dir * 128), BF16),
             pltpu.VMEM((n_mine * n_dir, 128), F32),
             pltpu.VMEM((tiles, n_mine, n_dir, 128), BF16),
@@ -344,13 +360,14 @@
             pltpu.SMEM((2 * n_dir, mirrors, 1, shard_rows), I32),
             pltpu.VMEM((n_dir * mirrors, 2 * subs), I32),
             pltpu.VMEM((shard_rows, n_dir, subs), I32),
-            pltpu.VMEM((8 * n_dir * mirrors, 1, 256), F32),
+            pltpu.VMEM((2 * n_dir * mirrors, 1, 256), F32),
             pltpu.VMEM((tiles * n_dir, 1, 128), F32),
-            dma((15, tiles)), dma((15, tiles)), dma((2,)), dma((2,)), dma, dma,
+            pltpu.VMEM((n_poke // 128, 128, 1), I32),
+            dma((15, tiles)), dma((15, tiles)), dma, dma, dma((mirrors,)), dma((mirrors,)), dma, dma,
             dma((n_dir, 2)), dma((n_dir, 2)), dma((n_dir,)), dma((n_dir,)),
             dma((n_dir, 2)), dma((n_dir, 2)), dma((tiles,)), dma((5,)),
         ],
-        compiler_params=pltpu.CompilerParams(collective_id=0, has_side_effects=True),
+        compiler_params=pltpu.CompilerParams(collective_id=0, has_side_effects=True, vmem_limit_bytes=62_500_000),
         name="window",
     )(
         influence.transpose(0, 1, 3, 2),

time: 89.3 us -> 82.8 us (0.927)
  Pallas kernels: 84.3 us -> 80.5 us
  local copies, waits for them, and re-layouts: 4.82 us -> 2.09 us
    pallas_call x1, Pallas kernels: 84.3 us -> 80.5 us  [shards(): pl.pallas_call(functools.partial(window_kernel, n_dir, n_row), out_shape=...]
    unnamed x1, local copies, waits for them, and re-layouts: 4.82 us -> 2.09 us
where the time goes in v4:
time: 82.8 us; the launch traced here: 82.6 us
  Pallas kernels  80.5 us (97%)
  local copies, waits for them, and re-layouts  2.09 us (3%)
    pallas_call x1, Pallas kernels, shards(): pl.pallas_call(functools.partial(window_kernel, n_dir, n_row), out_shape=...  80.5 us
    unnamed x1, local copies, waits for them, and re-layouts  2.09 us

profile of v4, /device:TPU:1, one launch (start us, length us, event | category | flops | bytes accessed | tf_op | source)
XLA Modules:
  0.0 82.6 jit_solution(3933236411037353412)
XLA Ops:
  0.0 80.5 %window.1 = bf16[27,8,10240]{2,1,0:T(8,128)(2,1)S(1)} custom-call(bf16[3,4,144,192]{3,2,1,0:T(8,128)(2,1)} %bitcast.5, s32[3,1,4]{2,1,0:T(1,128)} %bitcast.9, s32[3,1,160]{2,1,0:T(1,128)} %bitcast.8, s32[1,2,80]{2,1,0:T(2,128)} %valid.1, s32[3,48,48]{2,1,0:T(8,128)} %codes.1, s32[1,2048]{1,0:T(1,128)} %bitcast.6, s32[16,128]{1,0:T(8,128)} %bitcast.7), custom_call_target="tpu_custom_call" | custom-call | tf_op jit(solution)/shard_map/window/pallas_call | solution.py:340
  80.5 2.1 %copy.8 = bf16[27,8,10240]{2,1,0:T(8,128)(2,1)} copy(bf16[27,8,10240]{2,1,0:T(8,128)(2,1)S(1)} %window.1) | data formatting | bytes 8847360

commit v5 on v4

--- a/solution.py
+++ b/solution.py
@@ -21,6 +21,8 @@
 )
 PLACE = tuple((3 * w - 6) // 8 + 1 for w in range(12))
 REACHED = ((0, 5), (1, 4), (1, 5), (2, 5))
+ORDER = [(k, m) for m in (1, 2, 3, 4, 5) for k in range(3)] + [(k, m) for m in (0, 6) for k in range(3)]
+SOON = 768
 BF16, F32, I32 = jnp.bfloat16, jnp.float32, jnp.int32
 
 
@@ -34,7 +36,7 @@
 
 def sign_of(code_values, row_values):
     odd = jnp.bitwise_and(lax.population_count(jnp.bitwise_and(code_values, row_values)), 1)
-    return jnp.where(odd == 0, 1.0, -1.0).astype(BF16)
+    return jnp.where(odd == 0, 1.0, -1.0).astype(jnp.float8_e4m3fn)
 
 
 def dot(a, b):
@@ -45,10 +47,10 @@
     return jnp.right_shift(codes, 7).astype(F32).astype(BF16), jnp.bitwise_and(codes, 127).astype(F32).astype(BF16)
 
 
-def window_kernel(n_dir, n_row, own, foot_rows, foot_cols, valid, codes, pokes_lane, pokes_tile, out,
+def window_kernel(n_dir, n_row, own, foot_rows, foot_cols, valid, codes_in, pokes_lane_in, pokes_tile_in, out,
                   window, frames, sums, weights, staged, ready, left, right, gram, mine, local,
                   feet_land, cols_land, valid_land, feet, cols_mat, valid_mat, picks, mask,
-                  poke_cols, far_send, far_recv, halo_send, halo_recv, pair_send, pair_recv, relay_send, relay_recv,
+                  poke_cols, codes, pokes_lane, pokes_tile, far_send, far_recv, halo_send, halo_recv, pair_send, pair_recv, relay_send, relay_recv,
                   feet_send, feet_recv, cols_send, cols_recv, valid_send, valid_recv, keep_sem, own_sem):
     me_dir, me = lax.axis_index("dir"), lax.axis_index("row")
     core = lax.rem(me, 2)
@@ -87,41 +89,13 @@
         pltpu.make_async_copy(foot_cols, cols_land.at[me_dir], own_sem.at[2]),
         pltpu.make_async_copy(valid, valid_land.at[core * n_dir + me_dir], own_sem.at[3]),
     ]
-    for copy in keeps:
+    tables = [
+        pltpu.make_async_copy(codes_in, codes, own_sem.at[5]),
+        pltpu.make_async_copy(pokes_tile_in, pokes_tile, own_sem.at[6]),
+        pltpu.make_async_copy(pokes_lane_in, pokes_lane, own_sem.at[7]),
+    ]
+    for copy in keeps + tables:
         copy.start()
-
-    n_mine, n_poke = left.shape
-    n_local = right.shape[1]
-    table = [halves(codes[k]) for k in range(mirrors)]
-    at = iota((n_mine, 1), 0)
-    at = at + each * (over(at, each) + core)
-    at_row = over(at, NA)
-    at_col = at - NA * at_row
-    per_dir = mirrors * NAR // n_dir
-    upper = jnp.zeros((n_mine, NA), F32)
-    lower = jnp.zeros((n_mine, NA), F32)
-    for k in range(mirrors):
-        hot = (iota((n_mine, NAR), 1) == at_row + (per_dir * me_dir - NAR * k)).astype(F32).astype(BF16)
-        upper += dot(hot, table[k][0])
-        lower += dot(hot, table[k][1])
-    picked = jnp.where(iota((n_mine, NA), 1) == at_col, upper * 128.0 + lower, 0.0)
-    mine[...] = jnp.sum(picked, axis=1, keepdims=True).astype(I32)
-
-    lane = iota((1, n_local), 1)
-    block = over(lane, NA)
-    tile_of = (iota((NA, n_local), 0) == lane - NA * block).astype(F32).astype(BF16)
-    row_id = iota((NAR, n_local), 0)
-    found = jnp.zeros((1, n_local), F32)
-    for k in range(mirrors):
-        spread = dot(table[k][0], tile_of) * 128.0 + dot(table[k][1], tile_of)
-        wanted = jnp.where((block >= SPAN * k) & (block < SPAN * (k + 1)), block - SPAN * k + 3 * chip - 2, -1)
-        found += jnp.sum(jnp.where(row_id == wanted, spread, 0.0), axis=0, keepdims=True)
-    local[...] = found.astype(I32)
-
-    turned = jnp.transpose(pokes_tile[...])
-    for j in range(n_poke // 128):
-        poke_cols[j] = turned[:, j : j + 1]
-    frames[...] = jnp.zeros_like(frames)
 
     pl.semaphore_wait(barrier, 2 * n_dir + len(AROUND))
 
@@ -159,20 +133,59 @@
     for copy in small:
         copy.start()
 
-    @pl.loop(0, n_poke // 128)
-    def _(j):
-        part = pl.ds(pl.multiple_of(j * 128, 128), 128)
-        right[part, :] = sign_of(poke_cols[j], local[...])
+    for copy in tables:
+        copy.wait()
+
+    n_mine, n_poke = left.shape
+    n_local = right.shape[1]
+    table = [halves(codes[k]) for k in range(mirrors)]
+    at = iota((n_mine, 1), 0)
+    at = at + each * (over(at, each) + core)
+    at_row = over(at, NA)
+    at_col = at - NA * at_row
+    per_dir = mirrors * NAR // n_dir
+    upper = jnp.zeros((n_mine, NA), F32)
+    lower = jnp.zeros((n_mine, NA), F32)
+    for k in range(mirrors):
+        hot = (iota((n_mine, NAR), 1) == at_row + (per_dir * me_dir - NAR * k)).astype(F32).astype(BF16)
+        upper += dot(hot, table[k][0])
+        lower += dot(hot, table[k][1])
+    picked = jnp.where(iota((n_mine, NA), 1) == at_col, upper * 128.0 + lower, 0.0)
+    mine[...] = jnp.sum(picked, axis=1, keepdims=True).astype(I32)
+
+    lane = iota((1, n_local), 1)
+    block = over(lane, NA)
+    tile_of = (iota((NA, n_local), 0) == lane - NA * block).astype(F32).astype(BF16)
+    row_id = iota((NAR, n_local), 0)
+    found = jnp.zeros((1, n_local), F32)
+    for k in range(mirrors):
+        spread = dot(table[k][0], tile_of) * 128.0 + dot(table[k][1], tile_of)
+        third = over(block, mirrors)
+        band = jnp.where(third < SPAN - 2, third + 1, (SPAN - 1) * (third - (SPAN - 2)))
+        wanted = jnp.where(block - mirrors * third == k, band + 3 * chip - 2, -1)
+        found += jnp.sum(jnp.where(row_id == wanted, spread, 0.0), axis=0, keepdims=True)
+    local[...] = found.astype(I32)
+
+    turned = jnp.transpose(pokes_tile[...])
+    for j in range(n_poke // 128):
+        poke_cols[j] = turned[:, j : j + 1]
+    def right_of(columns):
+        @pl.loop(0, n_poke // 128)
+        def _(j):
+            part = pl.ds(pl.multiple_of(j * 128, 128), 128)
+            right[part, columns] = sign_of(poke_cols[j], local[:, columns])
+
+    right_of(slice(0, SOON))
 
     relay = remote(window.at[:, pl.ds(far_edge * core, REACH)], window.at[:, pl.ds(far_edge * core, REACH)],
                    relay_send, relay_recv, (me_dir, twin))
 
-    @pl.loop(0, n_mine // 48)
+    @pl.loop(0, n_mine // 144)
     def _(step):
-        part = pl.ds(pl.multiple_of(step * 48, 48), 48)
+        part = pl.ds(pl.multiple_of(step * 144, 144), 144)
         left[part, :] = sign_of(mine[part, :], pokes_lane[...])
 
-    gram[...] = dot(left[...], right[...]).astype(BF16)
+    gram[:, :SOON] = dot(left[...], right[:, :SOON]).astype(BF16)
 
     for copy in keeps:
         copy.wait()
@@ -223,7 +236,8 @@
                 start = start - lax.div(chip + 1, chips)
             part = pl.ds(start * NA if isinstance(start, int) else pl.multiple_of(start * NA, NA), slots)
             for k in range(mirrors):
-                frames[k, w, part, :] = window[k, w]
+                frames[k, w] = jnp.zeros(frames.shape[2:], BF16)
+                frames[k, w, part, :columns] = window[k, w]
 
     fill(range(REACH, far_edge))
 
@@ -243,49 +257,52 @@
             keep_sem.at[t],
         )
 
-    col_id = iota((columns, wide), 0).astype(F32)
+    col_id = iota((frames.shape[3], wide), 0).astype(F32).astype(BF16)
+    one, zero = jnp.ones((), BF16), jnp.zeros((), BF16)
     lane = iota((1, wide), 1)
     def sample(i):
         low, many = REACHED[i]
         turn = jnp.where(lane < 32 * i + subs, -1.0, 1.0)
+        turn, back = turn.astype(BF16), (-turn).astype(BF16)
         pick(i)
-
-        def framed(value):
-            blank = [jnp.zeros((n * NA, 128), F32) for n in (low, SPAN - low - many)]
-            pieces = [blank[0], value, blank[1]]
-            return jnp.concatenate([p for p in pieces if p.shape[0]], axis=0)
 
         @pl.loop(0, n_dir)
         def _(d):
             block = pl.ds(pl.multiple_of(d * 128, 128), 128)
             for k in range(mirrors):
-                later = picks[d * mirrors + k]
-                first = picks[(n_dir + d) * mirrors + k]
-                hot = jnp.where(col_id == later, 1.0, 0.0) + jnp.where(col_id == first, turn, 0.0)
-                hot = hot.astype(BF16)
-                terms = []
+                later = picks[d * mirrors + k].astype(BF16)
+                first = picks[(n_dir + d) * mirrors + k].astype(BF16)
+                hot = jnp.where(col_id == later, one, zero) + jnp.where(col_id == first, turn, zero)
+                picked = []
                 for a in range(2):
                     row = 2 * i + a
                     at = feet[row // rows * n_dir + d, k, 0, row % rows]
                     w = jnp.clip(at - 2 * rows * chip + REACH, 0, window_rows - 1)
-                    terms.append(dot(frames[k, w, pl.ds(low * NA, many * NA), :], hot))
-                part = terms[1] - terms[0] * turn
-                whole = pl.ds(k * frame, frame)
-                here, after = framed(part[:, :128]), framed(part[:, 128:])
-                if i == 1:
-                    sums[0, whole, block] = here
-                    sums[1, whole, block] = after
-                elif i == 0:
-                    weights[whole, block] = here.astype(BF16)
-                    sums[0, whole, block] += after
-                else:
-                    weights[whole, block] = (here + sums[1, whole, block]).astype(BF16)
-                    sums[1, whole, block] = after
-
-    def deliver(t):
+                    picked.append(frames[k, w, pl.ds(low * NA, many * NA), :])
+                part = dot(jnp.concatenate(picked, axis=1), jnp.concatenate([hot * back, hot], axis=0))
+                for n, (k_of, m) in enumerate(ORDER):
+                    if k_of != k:
+                        continue
+                    at = pl.ds(n * NA, NA)
+                    if low <= m < low + many:
+                        here = part[(m - low) * NA : (m - low + 1) * NA, :128]
+                        after = part[(m - low) * NA : (m - low + 1) * NA, 128:]
+                    else:
+                        here = after = jnp.zeros((NA, 128), F32)
+                    if i == 1:
+                        sums[0, at, block] = here
+                        sums[1, at, block] = after
+                    elif i == 0:
+                        weights[at, block] = here.astype(BF16)
+                        sums[0, at, block] += after
+                    else:
+                        weights[at, block] = (here + sums[1, at, block]).astype(BF16)
+                        sums[1, at, block] = after
+
+    def deliver(t, depth):
         @pl.loop(0, n_dir // 2)
         def _(c):
-            part = dot(gram[...], weights[:, pl.ds(pl.multiple_of(c * 256, 256), 256)])
+            part = dot(gram[:, :depth], weights[:depth, pl.ds(pl.multiple_of(c * 256, 256), 256)])
             for e in range(2):
                 d = 2 * c + e
                 staged[pl.ds(d, n_mine, stride=n_dir), :] = part[:, 128 * e : 128 * (e + 1)] * mask[t * n_dir + d]
@@ -306,17 +323,19 @@
     halo.wait()
     relay.start()
     sample(2)
-    deliver(2)
+    deliver(2, SOON)
     relay.wait()
+    right_of(slice(SOON, n_local))
+    gram[:, SOON:] = dot(left[...], right[:, SOON:]).astype(BF16)
     fill((0, 1, far_edge, far_edge + 1))
     sample(0)
-    deliver(0)
+    deliver(0, n_local)
     weights[...] = sums[0].astype(BF16)
-    deliver(1)
+    deliver(1, n_local)
     sample(3)
-    deliver(3)
+    deliver(3, n_local)
     weights[...] = sums[1].astype(BF16)
-    deliver(4)
+    deliver(4, n_local)
 
     for t in range(tiles):
         keep(t).wait()
@@ -340,17 +359,17 @@
     return pl.pallas_call(
         functools.partial(window_kernel, n_dir, n_row),
         out_shape=pltpu.VMEM((each, n_dir, lanes * chips), BF16),
-        in_specs=[ANY, ANY, ANY, ANY, VMEM, VMEM, VMEM],
+        in_specs=[ANY] * 7,
         out_specs=VMEM,
         scratch_shapes=[
             pltpu.VMEM((mirrors, window_rows, slots, columns), BF16),
-            pltpu.VMEM((mirrors, window_rows, SPAN * NA, columns), BF16),
+            pltpu.VMEM((mirrors, window_rows, SPAN * NA, 256), BF16),
             pltpu.VMEM((2, n_local, n_dir * 128), F32),
             pltpu.VMEM((n_local, n_dir * 128), BF16),
             pltpu.VMEM((n_mine * n_dir, 128), F32),
             pltpu.VMEM((tiles, n_mine, n_dir, 128), BF16),
-            pltpu.VMEM((n_mine, n_poke), BF16),
-            pltpu.VMEM((n_poke, n_local), BF16),
+            pltpu.VMEM((n_mine, n_poke), jnp.float8_e4m3fn),
+            pltpu.VMEM((n_poke, n_local), jnp.float8_e4m3fn),
             pltpu.VMEM((n_mine, n_local), BF16),
             pltpu.VMEM((n_mine, 1), I32),
             pltpu.VMEM((1, n_local), I32),
@@ -363,9 +382,12 @@
             pltpu.VMEM((2 * n_dir * mirrors, 1, 256), F32),
             pltpu.VMEM((tiles * n_dir, 1, 128), F32),
             pltpu.VMEM((n_poke // 128, 128, 1), I32),
+            pltpu.VMEM(actuator_codes.shape, I32),
+            pltpu.VMEM((1, n_poke), I32),
+            pltpu.VMEM((n_poke // 128, 128), I32),
             dma((15, tiles)), dma((15, tiles)), dma, dma, dma((mirrors,)), dma((mirrors,)), dma, dma,
             dma((n_dir, 2)), dma((n_dir, 2)), dma((n_dir,)), dma((n_dir,)),
-            dma((n_dir, 2)), dma((n_dir, 2)), dma((tiles,)), dma((5,)),
+            dma((n_dir, 2)), dma((n_dir, 2)), dma((tiles,)), dma((8,)),
         ],
         compiler_params=pltpu.CompilerParams(collective_id=0, has_side_effects=True, vmem_limit_bytes=62_500_000),
         name="window",

time: 82.8 us -> 81.5 us (0.984)
  Pallas kernels: 80.5 us -> 79.4 us
    pallas_call x1, Pallas kernels: 80.5 us -> 79.4 us  [shards(): pl.pallas_call(functools.partial(window_kernel, n_dir, n_row), out_shape=...]
where the time goes in v5:
time: 81.5 us
  Pallas kernels  79.4 us (97%)
  local copies, waits for them, and re-layouts  2.09 us (3%)
    pallas_call x1, Pallas kernels, shards(): pl.pallas_call(functools.partial(window_kernel, n_dir, n_row), out_shape=...  79.4 us
    unnamed x1, local copies, waits for them, and re-layouts  2.09 us

profile of v5, /device:TPU:1, one launch (start us, length us, event | category | flops | bytes accessed | tf_op | source)
XLA Modules:
  0.0 81.5 jit_solution(12720664047578016227)
XLA Ops:
  0.0 79.4 %window.1 = bf16[27,8,10240]{2,1,0:T(8,128)(2,1)S(1)} custom-call(bf16[3,4,144,192]{3,2,1,0:T(8,128)(2,1)} %bitcast.5, s32[3,1,4]{2,1,0:T(1,128)} %bitcast.9, s32[3,1,160]{2,1,0:T(1,128)} %bitcast.8, s32[1,2,80]{2,1,0:T(2,128)} %valid.1, s32[3,48,48]{2,1,0:T(8,128)} %codes_in.1, s32[1,2048]{1,0:T(1,128)} %bitcast.6, s32[16,128]{1,0:T(8,128)} %bitcast.7), custom_call_target="tpu_custom_call" | custom-call | tf_op jit(solution)/shard_map/window/pallas_call | solution.py:359
  79.4 2.1 %copy.8 = bf16[27,8,10240]{2,1,0:T(8,128)(2,1)} copy(bf16[27,8,10240]{2,1,0:T(8,128)(2,1)S(1)} %window.1) | data formatting | bytes 8847360
